TPU v7x, 512 devices: a whole 4x8x8 slice. The times are simulated.
512 devices in a mesh: rows: 128 (over z, x, y_hi, core), chan: 4 (over y_lo).
Axes of the slice: x: 4, y: 8 (y_hi: 2, y_lo: 4; y = y_hi * 4 + y_lo), z: 8, core: 2. Of those that a mesh axis runs over, the one named last changes fastest.
Arguments:
- za: bfloat16 [256, 48, 1024], P('rows', 'chan'), may hold values from -6 to 6
- zb: bfloat16 [256, 48, 1024], P('rows', 'chan'), may hold values from -6 to 6
- w_in: bfloat16 [3, 3, 48, 512], P(None, None, None, 'chan'), may hold values from -0.3125 to 0.3125
- b_in: float32 [512], P('chan'), may hold values from -3 to 3
- w_out: bfloat16 [3, 3, 512, 2, 48], P(None, None, 'chan'), may hold values from -0.09375 to 0.09375
- b_out: float32 [2, 48], replicated, may hold values from -3 to 3
- unmix: float32 [96, 96], replicated, may hold values from -0.625 to 0.625
- kern: float32 [3, 3, 96], replicated, may hold values from -1.4 to 1.4, as said below
Outputs:
- sample: float32 [256, 96, 1024], P('rows', 'chan')
Inputs may be any that keep to these rules, and one draw needn't show every extreme that they name: `kern`: for every channel the centre entry is positive and the eight other entries are negative with magnitudes summing to less than the centre.
All inputs are finite; a program needn't handle non-finite values.
Results may differ from a plain program's by a relative error of at most 0.0015.
Values may be sent and summed in bfloat16 or wider, within the bound.
A program may use at most 64 MiB of HBM per device.

v0:
```python
import math

import jax
import jax.numpy as jnp
from jax import lax
from jax.sharding import PartitionSpec as P

full_turn = 2.0 * math.pi


def extended(block, sides, width):
    for axis, dim in sides:
        count = lax.axis_size(axis)
        forward = [(i, i + 1) for i in range(count - 1)]
        backward = [(target, source) for source, target in forward]
        low = lax.ppermute(
            lax.slice_in_dim(block, block.shape[dim] - width, None, axis=dim), axis, forward
        )
        high = lax.ppermute(lax.slice_in_dim(block, 0, width, axis=dim), axis, backward)
        block = jnp.concatenate([low, block, high], axis=dim)
    return block


def conv_rows(source, weight):
    rows_out = source.shape[0] - 2
    width = source.shape[2]
    padded = jnp.pad(source, ((0, 0), (0, 0), (1, 1)))
    pieces = [
        padded[row_off : row_off + rows_out, :, col_off : col_off + width]
        for row_off in range(3)
        for col_off in range(3)
    ]
    stacked = jnp.stack(pieces, axis=1)
    taps = weight.reshape(9, weight.shape[2], weight.shape[3])
    return jnp.einsum("rkcw,kco->row", stacked, taps, preferred_element_type=jnp.float32)


def stencil_spectrum(kern, freq_rows, height, freq_cols, width):
    shape = (freq_rows.shape[0], kern.shape[2], freq_cols.shape[0])
    real_part = jnp.zeros(shape, jnp.float32)
    imag_part = jnp.zeros(shape, jnp.float32)
    for row_off in range(3):
        for col_off in range(3):
            phase_rows = (freq_rows * (row_off - 1) % height).astype(jnp.float32) * (
                full_turn / height
            )
            phase_cols = (freq_cols * (col_off - 1) % width).astype(jnp.float32) * (
                full_turn / width
            )
            phase = phase_rows[:, None, None] + phase_cols[None, None, :]
            weight = kern[row_off, col_off][None, :, None]
            real_part = real_part + weight * jnp.cos(phase)
            imag_part = imag_part + weight * jnp.sin(phase)
    return (real_part, imag_part)


def forward_cols(data, width):
    block_len = min(256, width)
    samples = jnp.arange(width, dtype=jnp.int32)
    real_blocks = []
    imag_blocks = []
    for block_idx in range(width // block_len):
        freqs = block_idx * block_len + jnp.arange(block_len, dtype=jnp.int32)
        angles = (samples[:, None] * freqs[None, :] % width).astype(jnp.float32) * (
            full_turn / width
        )
        real_blocks.append(
            jnp.einsum("rcw,wv->rcv", data, jnp.cos(angles), precision=lax.Precision.HIGHEST)
        )
        imag_blocks.append(
            -jnp.einsum("rcw,wv->rcv", data, jnp.sin(angles), precision=lax.Precision.HIGHEST)
        )
    return (jnp.concatenate(real_blocks, axis=2), jnp.concatenate(imag_blocks, axis=2))


def inverse_cols(real_part, imag_part, freq_of_pos, width):
    block_len = min(256, width)
    samples = jnp.arange(width, dtype=jnp.int32)
    total = jnp.zeros((real_part.shape[0], real_part.shape[1], width), jnp.float32)
    for block_idx in range(width // block_len):
        lower = block_idx * block_len
        freqs = freq_of_pos[lower : lower + block_len]
        angles = (freqs[:, None] * samples[None, :] % width).astype(jnp.float32) * (
            full_turn / width
        )
        total = total + jnp.einsum(
            "rcv,vw->rcw",
            real_part[:, :, lower : lower + block_len],
            jnp.cos(angles),
            precision=lax.Precision.HIGHEST,
        )
        total = total - jnp.einsum(
            "rcv,vw->rcw",
            imag_part[:, :, lower : lower + block_len],
            jnp.sin(angles),
            precision=lax.Precision.HIGHEST,
        )
    return total / width


def rows_transform(real_part, imag_part, height, sign):
    positions = jnp.arange(height, dtype=jnp.int32)
    angles = (positions[:, None] * positions[None, :] % height).astype(jnp.float32) * (
        full_turn / height
    )
    cosine = jnp.cos(angles)
    sine = jnp.sin(angles)

    def apply_table(values, table):
        return jnp.einsum("hcw,hu->ucw", values, table, precision=lax.Precision.HIGHEST)

    new_real = apply_table(real_part, cosine) + sign * apply_table(imag_part, sine)
    new_imag = apply_table(imag_part, cosine) - sign * apply_table(real_part, sine)
    return (new_real, new_imag)


def divide_symbol(real_part, imag_part, symbol_real, symbol_imag):
    denom = symbol_real * symbol_real + symbol_imag * symbol_imag
    return (
        (real_part * symbol_real + imag_part * symbol_imag) / denom,
        (imag_part * symbol_real - real_part * symbol_imag) / denom,
    )


def on_device(za, zb, w_in, b_in, w_out, b_out, unmix, kern):
    slab, quarter, width = za.shape
    hidden_local = w_in.shape[3]
    chans = unmix.shape[0]
    row_count = lax.axis_size("rows")
    chan_count = lax.axis_size("chan")
    row_idx = lax.axis_index("rows")
    chan_idx = lax.axis_index("chan")
    height = slab * row_count
    per_row = width // row_count
    rim_width = 1
    za_rim = extended(za, (("rows", 0),), rim_width)
    za_all = lax.all_gather(za_rim, "chan", axis=1, tiled=True)
    hidden = jax.nn.relu(conv_rows(za_all, w_in) + b_in[None, :, None])
    hidden_ext = extended(hidden.astype(jnp.bfloat16), (("rows", 0),), 1)
    arranged = (
        w_out.reshape(3, 3, hidden_local, 2, chan_count, quarter)
        .transpose(0, 1, 2, 4, 3, 5)
        .reshape(3, 3, hidden_local, chans)
    )
    share = lax.psum_scatter(
        conv_rows(hidden_ext, arranged).astype(jnp.bfloat16),
        "chan",
        scatter_dimension=1,
        tiled=True,
    ).astype(jnp.float32)
    bias_local = lax.dynamic_slice_in_dim(b_out, chan_idx * quarter, quarter, 1).reshape(
        2 * quarter
    )
    share = share + bias_local[None, :, None]
    coupled = (zb.astype(jnp.float32) - share[:, quarter:]) * jnp.exp(-jnp.tanh(share[:, :quarter]))
    joined = jnp.concatenate([za.astype(jnp.float32), coupled], axis=1)
    real_part, imag_part = forward_cols(joined, width)
    spectrum = lax.all_to_all(
        lax.all_to_all(
            jnp.stack([real_part, imag_part]), "rows", split_axis=3, concat_axis=1, tiled=True
        ),
        "chan",
        split_axis=3,
        concat_axis=2,
        tiled=True,
    )
    real_part, imag_part = rows_transform(spectrum[0], spectrum[1], height, 1.0)
    reordered = (
        unmix.reshape(chans, 2, chan_count, quarter).transpose(0, 2, 1, 3).reshape(chans, chans)
    )
    real_part = jnp.einsum("oc,ucw->uow", reordered, real_part, precision=lax.Precision.HIGHEST)
    imag_part = jnp.einsum("oc,ucw->uow", reordered, imag_part, precision=lax.Precision.HIGHEST)
    per_dev = per_row // chan_count
    freq_cols = row_idx * per_row + chan_idx * per_dev + jnp.arange(per_dev, dtype=jnp.int32)
    symbol_real, symbol_imag = stencil_spectrum(
        kern, jnp.arange(height, dtype=jnp.int32), height, freq_cols, width
    )
    real_part, imag_part = divide_symbol(real_part, imag_part, symbol_real, symbol_imag)
    real_part, imag_part = rows_transform(real_part, imag_part, height, -1.0)
    solved = jnp.stack([real_part, imag_part]) / height
    back = lax.all_to_all(
        lax.all_to_all(solved, "rows", split_axis=1, concat_axis=3, tiled=True),
        "chan",
        split_axis=2,
        concat_axis=3,
        tiled=True,
    )
    positions = jnp.arange(width, dtype=jnp.int32)
    freq_of_pos = (
        positions // per_dev % row_count * per_row
        + positions // (width // chan_count) * per_dev
        + positions % per_dev
    )
    return inverse_cols(back[0], back[1], freq_of_pos, width)


def solution(mesh):
    placed = (
        P("rows", "chan", None),
        P("rows", "chan", None),
        P(None, None, None, "chan"),
        P("chan"),
        P(None, None, "chan", None, None),
        P(),
        P(),
        P(),
    )
    return jax.shard_map(
        on_device, mesh=mesh, in_specs=placed, out_specs=P("rows", "chan", None), check_vma=False
    )
```

profile of v0, /device:TPU:1, one launch (start us, length us, event | category | flops | bytes accessed | tf_op | source)
XLA Modules:
  0.0 301.8 jit_solution(13705285724592824437)
XLA Ops:
  7.5 8.8 %collective-permute-start = (bf16[1,12,1024]{2,0,1:T(2,128)(2,1)S(1)}, bf16[1,12,1024]{2,0,1:T(2,128)(2,1)S(1)}, u32[]{:S(2)}, u32[]{:S(2)}) collective-permute-start(bf16[1,12,1024]{2,0,1:T(2,128)(2,1)S(1)} %get-tuple-element.11), channel_id=1, source_target_pairs={{0,4},{4,8},{8,12},{12,16},{16,20},{20,24},{24,28},{28,32},{32,36}... | collective-permute-start | bytes 73736 | tf_op jit(solution)/shard_map/ppermute | solution.py:16
  18.3 7.4 %collective-permute-done.1 = bf16[1,12,1024]{2,0,1:T(2,128)(2,1)S(1)} collective-permute-done((bf16[1,12,1024]{2,0,1:T(2,128)(2,1)S(1)}, bf16[1,12,1024]{2,0,1:T(2,128)(2,1)S(1)}, u32[]{:S(2)}, u32[]{:S(2)}) %collective-permute-start.1) | collective-permute-done | bytes 24608 | tf_op jit(solution)/shard_map/ppermute | solution.py:19
  26.6 11.5 %all_gather.3 = bf16[4,48,1024]{2,0,1:T(4,128)(2,1)S(1)} all-gather(bf16[4,12,1024]{2,0,1:T(4,128)(2,1)S(1)} %pad_maximum_fusion.4), channel_id=1, replica_groups=mesh['rows'=128,'chan'=4] {'chan'}, dimensions={1}, use_global_device_ids=true | all-gather | bytes 491520 | tf_op jit(solution)/shard_map/all_gather | solution.py:137
  40.0 5.7 %collective-permute-start.2 = (bf16[1,128,1024]{1,2,0:T(8,128)(2,1)S(1)}, bf16[1,128,1024]{1,2,0:T(8,128)(2,1)S(1)}, u32[]{:S(2)}, u32[]{:S(2)}) collective-permute-start(bf16[1,128,1024]{1,2,0:T(8,128)(2,1)S(1)} %get-tuple-element.5), channel_id=1, source_target_pairs={{0,4},{4,8},{8,12},{12,16},{16,20},{20,24},{24,28},{28,32},{32,36}... | collective-permute-start | bytes 786440 | tf_op jit(solution)/shard_map/ppermute | solution.py:16
  48.1 3.2 %collective-permute-done.2 = bf16[1,128,1024]{1,2,0:T(8,128)(2,1)S(1)} collective-permute-done((bf16[1,128,1024]{1,2,0:T(8,128)(2,1)S(1)}, bf16[1,128,1024]{1,2,0:T(8,128)(2,1)S(1)}, u32[]{:S(2)}, u32[]{:S(2)}) %collective-permute-start.2) | collective-permute-done | bytes 262176 | tf_op jit(solution)/shard_map/ppermute | solution.py:16
  51.3 6.1 %collective-permute-done.3 = bf16[1,128,1024]{1,2,0:T(8,128)(2,1)S(1)} collective-permute-done((bf16[1,128,1024]{1,2,0:T(8,128)(2,1)S(1)}, bf16[1,128,1024]{1,2,0:T(8,128)(2,1)S(1)}, u32[]{:S(2)}, u32[]{:S(2)}) %collective-permute-start.3) | collective-permute-done | bytes 262176 | tf_op jit(solution)/shard_map/ppermute | solution.py:19
  61.7 35.0 %reduce-scatter.4.cloned.1.call-done = bf16[24,2048]{1,0:T(8,128)(2,1)} async-done(((bf16[96,2048]{1,0:T(8,128)(2,1)}), bf16[24,2048]{1,0:T(8,128)(2,1)}) %reduce-scatter.4.cloned.1.call-update) | async-done | bytes 98320
  97.9 4.5 %convolution_negate_fusion = f32[2,24,256]{2,1,0:T(8,128)S(1)} fusion(f32[2,24,1024]{2,1,0:T(8,128)S(1)} %pad_maximum_fusion.3, s32[256]{0:T(256)S(1)} %iota_add_fusion), kind=kOutput, calls=%fused_computation.56 | convolution fusion | flops 154677248 | bytes 246784 | tf_op jit(solution)/shard_map/rcw,wv->rcv/dot_general | solution.py:71
  102.4 4.7 %fusion.53 = f32[2,24,256]{2,1,0:T(8,128)S(1)} fusion(f32[2,24,1024]{2,1,0:T(8,128)S(1)} %pad_maximum_fusion.3, s32[256]{0:T(256)S(1)} %iota_add_fusion), kind=kOutput, calls=%fused_computation.99 | convolution fusion | flops 154664960 | bytes 246784 | tf_op jit(solution)/shard_map/rcw,wv->rcv/dot_general | solution.py:68
  107.0 4.5 %convolution_negate_fusion.1 = f32[2,24,256]{2,1,0:T(8,128)S(1)} fusion(f32[2,24,1024]{2,1,0:T(8,128)S(1)} %pad_maximum_fusion.3, s32[256]{0:T(256)S(1)} %iota_add_fusion.1), kind=kOutput, calls=%fused_computation.57 | convolution fusion | flops 154677248 | bytes 246784 | tf_op jit(solution)/shard_map/rcw,wv->rcv/dot_general | solution.py:71
  111.5 4.5 %fusion.55 = f32[2,24,256]{2,1,0:T(8,128)S(1)} fusion(f32[2,24,1024]{2,1,0:T(8,128)S(1)} %pad_maximum_fusion.3, s32[256]{0:T(256)S(1)} %iota_add_fusion.1), kind=kOutput, calls=%fused_computation.101 | convolution fusion | flops 154664960 | bytes 246784 | tf_op jit(solution)/shard_map/rcw,wv->rcv/dot_general | solution.py:68
  116.0 5.0 %convolution_negate_fusion.2 = f32[2,24,256]{2,1,0:T(8,128)S(1)} fusion(f32[2,24,1024]{2,1,0:T(8,128)S(1)} %pad_maximum_fusion.3, s32[256]{0:T(256)S(1)} %iota_add_fusion.2), kind=kOutput, calls=%fused_computation.58 | convolution fusion | flops 154677248 | bytes 246784 | tf_op jit(solution)/shard_map/rcw,wv->rcv/dot_general | solution.py:71
  121.0 4.5 %fusion.57 = f32[2,24,256]{2,1,0:T(8,128)S(1)} fusion(f32[2,24,1024]{2,1,0:T(8,128)S(1)} %pad_maximum_fusion.3, s32[256]{0:T(256)S(1)} %iota_add_fusion.2), kind=kOutput, calls=%fused_computation.103 | convolution fusion | flops 154664960 | bytes 246784 | tf_op jit(solution)/shard_map/rcw,wv->rcv/dot_general | solution.py:68
  125.4 4.5 %convolution_negate_fusion.3 = f32[2,24,256]{2,1,0:T(8,128)S(1)} fusion(f32[2,24,1024]{2,1,0:T(8,128)S(1)} %pad_maximum_fusion.3), kind=kOutput, calls=%fused_computation.59 | convolution fusion | flops 154677248 | bytes 245760 | tf_op jit(solution)/shard_map/rcw,wv->rcv/dot_general | solution.py:71
  129.9 4.6 %fusion.59 = f32[2,24,256]{2,1,0:T(8,128)S(1)} fusion(f32[2,24,1024]{2,1,0:T(8,128)S(1)} %pad_maximum_fusion.3), kind=kOutput, calls=%fused_computation.105 | convolution fusion | flops 154664960 | bytes 245760 | tf_op jit(solution)/shard_map/rcw,wv->rcv/dot_general | solution.py:68
  136.0 4.5 %reshape.502 = f32[128,1,768]{2,1,0:T(1,128)} reshape(f32[1024,2,2,24]{3,2,1,0:T(2,128)S(1)} %bitcast.271) | data formatting | bytes 786432
  140.6 15.9 %all-to-all-start = ((f32[128,1,768]{2,1,0:T(1,128)}), f32[128,1,768]{2,1,0:T(1,128)S(1)}, u32[]{:S(2)}, u32[]{:S(2)}) async-start(f32[128,1,768]{2,1,0:T(1,128)} %reshape.502), calls=%async_computation | async-start | bytes 786432 | tf_op jit(solution)/shard_map/all_to_all | solution.py:159
  156.6 18.5 %all-to-all-done = f32[128,1,768]{2,1,0:T(1,128)S(1)} async-done(((f32[128,1,768]{2,1,0:T(1,128)}), f32[128,1,768]{2,1,0:T(1,128)S(1)}, u32[]{:S(2)}, u32[]{:S(2)}) %all-to-all-start) | async-done | bytes 393248 | tf_op jit(solution)/shard_map/all_to_all | solution.py:159
  177.2 3.4 %reshape.503 = f32[1024,2,2,24]{3,2,1,0:T(2,128)S(1)} reshape(f32[128,768]{1,0:T(8,128)S(1)} %reduce) | data formatting | bytes 786432
  182.4 5.2 %all-to-all-start.1 = ((f32[2,256,24,8]{1,2,0,3:T(8,128)}), f32[2,256,24,8]{1,2,0,3:T(8,128)S(1)}, u32[]{:S(2)}, u32[]{:S(2)}) async-start(f32[2,256,24,8]{1,2,0,3:T(8,128)} %copy.72), calls=%async_computation.1 | async-start | bytes 786432 | tf_op jit(solution)/shard_map/all_to_all | solution.py:158
  188.0 10.4 %all-to-all-done.1 = f32[2,256,24,8]{1,2,0,3:T(8,128)S(1)} async-done(((f32[2,256,24,8]{1,2,0,3:T(8,128)}), f32[2,256,24,8]{1,2,0,3:T(8,128)S(1)}, u32[]{:S(2)}, u32[]{:S(2)}) %all-to-all-start.1) | async-done | bytes 393248 | tf_op jit(solution)/shard_map/all_to_all | solution.py:158
  211.0 28.9 %all_to_all.66 = f32[2,256,96,2]{2,3,0,1:T(2,128)S(1)} all-to-all(f32[2,256,96,2]{2,3,0,1:T(2,128)S(1)} %copy.80), channel_id=1, replica_groups=mesh['rows'=128,'chan'=4] {'rows'}, dimensions={1} | all-to-all | bytes 786432 | tf_op jit(solution)/shard_map/all_to_all | solution.py:182
  241.3 3.5 %all-to-all-start.3 = ((f32[2,2,96,256]{3,1,0,2:T(2,128)}), f32[2,2,96,256]{3,1,0,2:T(2,128)S(1)}, u32[]{:S(2)}, u32[]{:S(2)}) async-start(f32[2,2,96,256]{3,1,0,2:T(2,128)} %copy.83), calls=%async_computation.3 | async-start | bytes 786432 | tf_op jit(solution)/shard_map/all_to_all | solution.py:181
  244.8 11.2 %all-to-all-done.3 = f32[2,2,96,256]{3,1,0,2:T(2,128)S(1)} async-done(((f32[2,2,96,256]{3,1,0,2:T(2,128)}), f32[2,2,96,256]{3,1,0,2:T(2,128)S(1)}, u32[]{:S(2)}, u32[]{:S(2)}) %all-to-all-start.3) | async-done | bytes 393248 | tf_op jit(solution)/shard_map/all_to_all | solution.py:181
  256.5 4.6 %fusion.47 = f32[2,24,1024]{2,1,0:T(8,128)S(1)} fusion(s32[256]{0:T(256)S(1)} %get-tuple-element.25, f32[2,24,1024]{2,1,0:T(8,128)S(1)} %squeeze.14), kind=kOutput, calls=%fused_computation.93 | convolution fusion | flops 154664960 | bytes 246784 | tf_op jit(solution)/shard_map/rcv,vw->rcw/dot_general | solution.py:86
  261.1 4.6 %convolution_subtract_fusion.4 = f32[2,24,1024]{2,1,0:T(8,128)S(1)} fusion(f32[2,24,1024]{2,1,0:T(8,128)S(1)} %fusion.47, s32[256]{0:T(256)S(1)} %get-tuple-element.25, f32[2,24,1024]{2,1,0:T(8,128)S(1)} %squeeze.15), kind=kOutput, calls=%fused_computation.52 | convolution fusion | flops 154714112 | bytes 443392 | tf_op jit(solution)/shard_map/rcv,vw->rcw/dot_general | solution.py:92
  265.8 5.0 %convolution_add_fusion.3 = f32[2,24,1024]{2,1,0:T(8,128)S(1)} fusion(f32[2,24,1024]{2,1,0:T(8,128)S(1)} %convolution_subtract_fusion.4, s32[256]{0:T(256)S(1)} %get-tuple-element.24, f32[2,24,1024]{2,1,0:T(8,128)S(1)} %squeeze.14), kind=kOutput, calls=%fused_computation.51 | convolution fusion | flops 154714112 | bytes 443392 | tf_op jit(solution)/shard_map/rcv,vw->rcw/dot_general | solution.py:86
  270.8 4.6 %convolution_subtract_fusion.3 = f32[2,24,1024]{2,1,0:T(8,128)S(1)} fusion(f32[2,24,1024]{2,1,0:T(8,128)S(1)} %convolution_add_fusion.3, s32[256]{0:T(256)S(1)} %get-tuple-element.24, f32[2,24,1024]{2,1,0:T(8,128)S(1)} %squeeze.15), kind=kOutput, calls=%fused_computation.50 | convolution fusion | flops 154714112 | bytes 443392 | tf_op jit(solution)/shard_map/rcv,vw->rcw/dot_general | solution.py:92
  275.4 4.6 %convolution_add_fusion.2 = f32[2,24,1024]{2,1,0:T(8,128)S(1)} fusion(f32[2,24,1024]{2,1,0:T(8,128)S(1)} %convolution_subtract_fusion.3, s32[256]{0:T(256)S(1)} %get-tuple-element.23, f32[2,24,1024]{2,1,0:T(8,128)S(1)} %squeeze.14), kind=kOutput, calls=%fused_computation.49 | convolution fusion | flops 154714112 | bytes 443392 | tf_op jit(solution)/shard_map/rcv,vw->rcw/dot_general | solution.py:86
  280.0 4.8 %convolution_subtract_fusion.2 = f32[2,24,1024]{2,1,0:T(8,128)S(1)} fusion(f32[2,24,1024]{2,1,0:T(8,128)S(1)} %convolution_add_fusion.2, s32[256]{0:T(256)S(1)} %get-tuple-element.23, f32[2,24,1024]{2,1,0:T(8,128)S(1)} %squeeze.15), kind=kOutput, calls=%fused_computation.48 | convolution fusion | flops 154714112 | bytes 443392 | tf_op jit(solution)/shard_map/rcv,vw->rcw/dot_general | solution.py:92
  284.8 4.6 %convolution_add_fusion.1 = f32[2,24,1024]{2,1,0:T(8,128)S(1)} fusion(f32[2,24,1024]{2,1,0:T(8,128)S(1)} %convolution_subtract_fusion.2, s32[256]{0:T(256)S(1)} %get-tuple-element.22, f32[2,24,1024]{2,1,0:T(8,128)S(1)} %squeeze.14), kind=kOutput, calls=%fused_computation.47 | convolution fusion | flops 154714112 | bytes 443392 | tf_op jit(solution)/shard_map/rcv,vw->rcw/dot_general | solution.py:86
  289.5 5.3 %fusion.13 = f32[2,24,1024]{2,1,0:T(8,128)} fusion(f32[2,24,1024]{2,1,0:T(8,128)S(1)} %convolution_add_fusion.1, s32[256]{0:T(256)S(1)} %get-tuple-element.22, f32[2,24,1024]{2,1,0:T(8,128)S(1)} %squeeze.15), kind=kOutput, calls=%fused_computation.55 | convolution fusion | flops 154763264 | bytes 443392 | tf_op jit(solution)/shard_map/rcv,vw->rcw/dot_general | solution.py:92
  (110 shorter events, 33.4 us)
Async XLA Ops:
  6.5 32.5 %copy-start = (bf16[3,3,48,128]{3,2,1,0:T(8,128)(2,1)S(1)}, bf16[3,3,48,128]{3,2,1,0:T(8,128)(2,1)}, u32[]{:S(2)}) copy-start(bf16[3,3,48,128]{3,2,1,0:T(8,128)(2,1)} %param.10) | copy-start | bytes 331780
  6.5 90.2 %reduce-scatter.4.cloned.1.call-start = ((), (), s32[]{:S(2)}) async-start(), calls=%async_computation.5 | async-start | bytes 491520
  7.5 10.8 %collective-permute-start = (bf16[1,12,1024]{2,0,1:T(2,128)(2,1)S(1)}, bf16[1,12,1024]{2,0,1:T(2,128)(2,1)S(1)}, u32[]{:S(2)}, u32[]{:S(2)}) collective-permute-start(bf16[1,12,1024]{2,0,1:T(2,128)(2,1)S(1)} %get-tuple-element.11), channel_id=1, source_target_pairs={{0,4},{4,8},{8,12},{12,16},{16,20},{20,24},{24,28},{28,32},{32,36}... | collective-permute-start | bytes 73736 | tf_op jit(solution)/shard_map/ppermute | solution.py:16
  16.3 9.3 %collective-permute-start.1 = (bf16[1,12,1024]{2,0,1:T(2,128)(2,1)S(1)}, bf16[1,12,1024]{2,0,1:T(2,128)(2,1)S(1)}, u32[]{:S(2)}, u32[]{:S(2)}) collective-permute-start(bf16[1,12,1024]{2,0,1:T(2,128)(2,1)S(1)} %get-tuple-element.12), channel_id=1, source_target_pairs={{4,0},{8,4},{12,8},{16,12},{20,16},{24,20},{28,24},{32,28},{36,32}... | collective-permute-start | bytes 73736 | tf_op jit(solution)/shard_map/ppermute | solution.py:19
  38.4 0.7 copy-start.7
  39.1 8.7 %copy-start.2 = (bf16[3,3,128,2,48]{2,4,3,1,0:T(8,128)(2,1)S(1)}, bf16[3,3,128,2,48]{2,4,3,1,0:T(8,128)(2,1)}, u32[]{:S(2)}) copy-start(bf16[3,3,128,2,48]{2,4,3,1,0:T(8,128)(2,1)} %param.12) | copy-start | bytes 663556
  40.0 11.3 %collective-permute-start.2 = (bf16[1,128,1024]{1,2,0:T(8,128)(2,1)S(1)}, bf16[1,128,1024]{1,2,0:T(8,128)(2,1)S(1)}, u32[]{:S(2)}, u32[]{:S(2)}) collective-permute-start(bf16[1,128,1024]{1,2,0:T(8,128)(2,1)S(1)} %get-tuple-element.5), channel_id=1, source_target_pairs={{0,4},{4,8},{8,12},{12,16},{16,20},{20,24},{24,28},{28,32},{32,36}... | collective-permute-start | bytes 786440 | tf_op jit(solution)/shard_map/ppermute | solution.py:16
  45.7 11.7 %collective-permute-start.3 = (bf16[1,128,1024]{1,2,0:T(8,128)(2,1)S(1)}, bf16[1,128,1024]{1,2,0:T(8,128)(2,1)S(1)}, u32[]{:S(2)}, u32[]{:S(2)}) collective-permute-start(bf16[1,128,1024]{1,2,0:T(8,128)(2,1)S(1)} %get-tuple-element.6), channel_id=1, source_target_pairs={{4,0},{8,4},{12,8},{16,12},{20,16},{24,20},{28,24},{32,28},{36,32}... | collective-permute-start | bytes 786440 | tf_op jit(solution)/shard_map/ppermute | solution.py:19
  60.2 1.3 copy-start.6
  60.2 1.5 copy-start.1
  60.2 37.6 %copy-start.3 = (bf16[2,12,1024]{2,0,1:T(2,128)(2,1)S(1)}, bf16[2,12,1024]{2,0,1:T(2,128)(2,1)}, u32[]{:S(2)}) copy-start(bf16[2,12,1024]{2,0,1:T(2,128)(2,1)} %param.9) | copy-start | bytes 147460
  136.0 20.6 %copy-start.5 = (f32[3,3,96]{2,1,0:T(4,128)S(1)}, f32[3,3,96]{2,1,0:T(4,128)}, u32[]{:S(2)}) copy-start(f32[3,3,96]{2,1,0:T(4,128)} %param.15) | copy-start | bytes 10372
  140.6 34.6 %all-to-all-start = ((f32[128,1,768]{2,1,0:T(1,128)}), f32[128,1,768]{2,1,0:T(1,128)S(1)}, u32[]{:S(2)}, u32[]{:S(2)}) async-start(f32[128,1,768]{2,1,0:T(1,128)} %reshape.502), calls=%async_computation | async-start | bytes 786432 | tf_op jit(solution)/shard_map/all_to_all | solution.py:159
  180.9 6.7 %copy-start.4 = (f32[96,96]{1,0:T(8,128)S(1)}, f32[96,96]{1,0:T(8,128)}, u32[]{:S(2)}) copy-start(f32[96,96]{1,0:T(8,128)} %param.14) | copy-start | bytes 110596
  182.4 16.0 %all-to-all-start.1 = ((f32[2,256,24,8]{1,2,0,3:T(8,128)}), f32[2,256,24,8]{1,2,0,3:T(8,128)S(1)}, u32[]{:S(2)}, u32[]{:S(2)}) async-start(f32[2,256,24,8]{1,2,0,3:T(8,128)} %copy.72), calls=%async_computation.1 | async-start | bytes 786432 | tf_op jit(solution)/shard_map/all_to_all | solution.py:158
  241.3 14.7 %all-to-all-start.3 = ((f32[2,2,96,256]{3,1,0,2:T(2,128)}), f32[2,2,96,256]{3,1,0,2:T(2,128)S(1)}, u32[]{:S(2)}, u32[]{:S(2)}) async-start(f32[2,2,96,256]{3,1,0,2:T(2,128)} %copy.83), calls=%async_computation.3 | async-start | bytes 786432 | tf_op jit(solution)/shard_map/all_to_all | solution.py:181
Sparse Core Ops, SparseCore 0:
  61.6 35.0 reduce-scatter.3
where the time goes:
time: 305 us; the launch traced here: 302 us
  waiting for transfers between devices  91.8 us (30%)
  matrix products  88.9 us (29%)
  starting transfers between devices  43.1 us (14%)
  blocking collectives  40.4 us (13%)
  local copies, waits for them, and re-layouts  19.2 us (6%)
  between operations  14.4 us (5%)
  other arithmetic  4.03 us (1%)
    unnamed x2, waiting for transfers between devices  35.1 us
    all_to_all x1, blocking collectives, on_device(): lax.all_to_all(solved, 'rows', split_axis=1, concat_axis=3, tiled=True)  28.9 us
    dot_general x4, matrix products, inverse_cols(): jnp.einsum('rcv,vw->rcw', imag_part[:, :, lower:lower + block_len], jnp.s...  19.4 us
    dot_general x4, matrix products, inverse_cols(): jnp.einsum('rcv,vw->rcw', real_part[:, :, lower:lower + block_len], jnp.c...  18.8 us
    all_to_all x1, waiting for transfers between devices, on_device(): lax.all_to_all(jnp.stack([real_part, imag_part]), 'rows', split_axis=3, c...  18.5 us
    dot_general x4, matrix products, forward_cols(): jnp.einsum('rcw,wv->rcv', data, jnp.sin(angles), precision=lax.Precision....  18.4 us
    dot_general x4, matrix products, forward_cols(): jnp.einsum('rcw,wv->rcv', data, jnp.cos(angles), precision=lax.Precision....  18.2 us
    all_to_all x1, starting transfers between devices, on_device(): lax.all_to_all(jnp.stack([real_part, imag_part]), 'rows', split_axis=3, c...  15.9 us
  transfers between devices with their start and end apart: 8, of which 7 were waited for; matrix products, arithmetic and copies ran while one was open for 0% of the time, Pallas kernels for 0%

commit v1 on v0

v1 whole, which is shorter than its diff:
```python
import math

import jax
import jax.numpy as jnp
import numpy as np
from jax import lax
from jax.experimental import pallas as pl
from jax.experimental.pallas import tpu as pltpu
from jax.sharding import PartitionSpec as P

full_turn = 2.0 * math.pi
vmem = pl.BlockSpec(memory_space=pltpu.VMEM)
mesh_ids = pl.DeviceIdType.MESH


def swap_kernel(axis, count, x_ref, out_ref, send_sem, recv_sem, own_sem):
    me_row = lax.axis_index("rows")
    me_chan = lax.axis_index("chan")
    me = me_row if axis == "rows" else me_chan

    def place(peer):
        return (peer, me_chan) if axis == "rows" else (me_row, peer)

    barrier = pltpu.get_barrier_semaphore()

    def greet(step, carry):
        pl.semaphore_signal(
            barrier, inc=1, device_id=place(lax.rem(me + step, count)), device_id_type=mesh_ids
        )
        return carry

    lax.fori_loop(1, count, greet, 0)
    own = pltpu.make_async_copy(x_ref.at[me], out_ref.at[me], own_sem)
    own.start()
    pl.semaphore_wait(barrier, count - 1)

    def copy(step):
        peer = lax.rem(me + step, count)
        return pltpu.make_async_remote_copy(
            src_ref=x_ref.at[peer],
            dst_ref=out_ref.at[me],
            send_sem=send_sem.at[step],
            recv_sem=recv_sem.at[step],
            device_id=place(peer),
            device_id_type=mesh_ids,
        )

    def start(step, carry):
        copy(step).start()
        return carry

    def finish(step, carry):
        copy(step).wait()
        return carry

    lax.fori_loop(1, count, start, 0)
    own.wait()
    lax.fori_loop(1, count, finish, 0)


def swap(x, axis, ident):
    count = x.shape[0]

    def kernel(*refs):
        swap_kernel(axis, count, *refs)

    return pl.pallas_call(
        kernel,
        out_shape=jax.ShapeDtypeStruct(x.shape, x.dtype),
        in_specs=[vmem],
        out_specs=vmem,
        scratch_shapes=[
            pltpu.SemaphoreType.DMA((count,)),
            pltpu.SemaphoreType.DMA((count,)),
            pltpu.SemaphoreType.DMA,
        ],
        compiler_params=pltpu.CompilerParams(collective_id=ident, has_side_effects=True),
        name="swap_" + axis + str(ident),
    )(x)


def gather_kernel(rows, chans, za_ref, zb_ref, out_ref, zb_out, sems_a, sems_b, own_sem):
    me_row = lax.axis_index("rows")
    me_chan = lax.axis_index("chan")
    barrier = pltpu.get_barrier_semaphore()
    peers = [(dr, dc) for dr in (0, 1, 2) for dc in range(chans) if (dr, dc) != (1, 0)]

    def place(dr, dc):
        return (lax.rem(me_row + dr + rows - 1, rows), lax.rem(me_chan + dc, chans))

    for dr, dc in peers:
        pl.semaphore_signal(barrier, inc=1, device_id=place(dr, dc), device_id_type=mesh_ids)
    own = pltpu.make_async_copy(za_ref, out_ref.at[1, me_chan], own_sem.at[0])
    own.start()
    own_b = pltpu.make_async_copy(zb_ref.at[me_chan], zb_out.at[me_chan], own_sem.at[1])
    own_b.start()
    pl.semaphore_wait(barrier, len(peers))
    copies = []
    for idx, (dr, dc) in enumerate(peers):
        copies.append(
            pltpu.make_async_remote_copy(
                src_ref=za_ref,
                dst_ref=out_ref.at[2 - dr, me_chan],
                send_sem=sems_a.at[0, idx],
                recv_sem=sems_a.at[1, idx],
                device_id=place(dr, dc),
                device_id_type=mesh_ids,
            )
        )
    for dc in range(1, chans):
        peer = lax.rem(me_chan + dc, chans)
        copies.append(
            pltpu.make_async_remote_copy(
                src_ref=zb_ref.at[peer],
                dst_ref=zb_out.at[me_chan],
                send_sem=sems_b.at[0, dc],
                recv_sem=sems_b.at[1, dc],
                device_id=(me_row, peer),
                device_id_type=mesh_ids,
            )
        )
    for one in copies:
        one.start()
    own.wait()
    own_b.wait()
    for one in copies:
        one.wait()


def gather(za, zb_cols, rows, chans):
    def kernel(*refs):
        gather_kernel(rows, chans, *refs)

    return pl.pallas_call(
        kernel,
        out_shape=(
            jax.ShapeDtypeStruct((3, chans) + za.shape, za.dtype),
            jax.ShapeDtypeStruct(zb_cols.shape, zb_cols.dtype),
        ),
        in_specs=[vmem, vmem],
        out_specs=(vmem, vmem),
        scratch_shapes=[
            pltpu.SemaphoreType.DMA((2, 3 * chans)),
            pltpu.SemaphoreType.DMA((2, chans)),
            pltpu.SemaphoreType.DMA((2,)),
        ],
        compiler_params=pltpu.CompilerParams(collective_id=0, has_side_effects=True),
        name="gather_latents",
    )(za, zb_cols)


def conv_rows(source, weight):
    rows_out = source.shape[0] - 2
    width = source.shape[2]
    padded = jnp.pad(source, ((0, 0), (0, 0), (1, 1)))
    pieces = [
        padded[row_off : row_off + rows_out, :, col_off : col_off + width]
        for row_off in range(3)
        for col_off in range(3)
    ]
    stacked = jnp.stack(pieces, axis=1)
    taps = weight.reshape(9, weight.shape[2], weight.shape[3])
    return jnp.einsum("rkcw,kco->row", stacked, taps, preferred_element_type=jnp.float32)


def halves(values):
    high = lax.reduce_precision(values, 8, 7)
    return high.astype(jnp.bfloat16), (values - high).astype(jnp.bfloat16)


def column_tables(width, group):
    pos = np.arange(width)
    part = pos // group % 2
    slot = pos // (2 * group) * group + pos % group
    first = slot == 0
    freq = np.where(first & (part == 1), width // 2, slot)
    shift = np.where(first, 0, part) * (math.pi / 2)
    fine = 32
    outer = (np.arange(width // fine) * fine)[:, None] * freq[None, :] % width * (full_turn / width)
    inner = np.arange(fine)[:, None] * freq[None, :] % width * (full_turn / width) + shift[None, :]
    consts = [f(a).astype(np.float32) for a in (outer, inner) for f in (np.cos, np.sin)]
    cos_o, sin_o, cos_i, sin_i = lax.optimization_barrier(tuple(jnp.asarray(c) for c in consts))
    table = cos_o[:, None, :] * cos_i[None] - sin_o[:, None, :] * sin_i[None]
    table = table.reshape(width, width)
    sign = np.where(first, 0.0, 1.0 - 2.0 * part).astype(np.float32)
    weight = np.where(first, 1.0, 2.0).astype(np.float32)
    return halves(table), freq, sign, weight


def dot3(left, right_halves, contract):
    high, low = halves(left)
    right_high, right_low = right_halves
    count = left.shape[0]

    def dot(a, b):
        return lax.dot_general(
            a, b, (((1,), (contract,)), ((), ())), preferred_element_type=jnp.float32
        )

    both = dot(jnp.concatenate([high, low], axis=0), right_high)
    return both[:count] + both[count:] + dot(high, right_low)


def on_device(za, zb, w_in, b_in, w_out, b_out, unmix, kern):
    slab, quarter, width = za.shape
    hidden_local = w_in.shape[3]
    chans = unmix.shape[0]
    half = chans // 2
    rows = lax.axis_size("rows")
    groups = lax.axis_size("chan")
    row_idx = lax.axis_index("rows")
    chan_idx = lax.axis_index("chan")
    height = slab * rows
    block = width // groups
    mine = chans // groups
    lanes = 64
    freq_groups = width // lanes
    chan_groups = rows // freq_groups
    triple = mine // chan_groups

    table, freq, sign, weight = column_tables(width, lanes // 2)

    zb_cols = zb.reshape(slab, quarter, groups, block).transpose(2, 0, 1, 3)
    za_got, zb_got = gather(za, zb_cols, rows, groups)
    za_ext = za_got.transpose(0, 2, 1, 3, 4).reshape(3 * slab, half, width)
    ext_rows = row_idx * slab - slab + jnp.arange(3 * slab, dtype=jnp.int32)
    inside = (ext_rows >= 0) & (ext_rows < height)
    za_ext = jnp.where(inside[:, None, None], za_ext, jnp.zeros((), za.dtype))
    hidden = jax.nn.relu(conv_rows(za_ext, w_in) + b_in[None, :, None])
    hidden = jnp.where(inside[1:-1][:, None, None], hidden, 0.0).astype(jnp.bfloat16)
    w_flat = w_out.reshape(3, 3, hidden_local, chans)
    share = conv_rows(hidden, w_flat).astype(jnp.bfloat16)
    share = share.reshape(slab, chans, groups, block).transpose(2, 0, 1, 3)
    raw = jnp.sum(swap(share, "chan", 1).astype(jnp.float32), axis=0)
    raw = raw + b_out.reshape(chans)[None, :, None]
    latent = zb_got.transpose(1, 0, 2, 3).reshape(slab, half, block).astype(jnp.float32)
    coupled = (latent - raw[:, half:]) * jnp.exp(-jnp.tanh(raw[:, :half]))
    za_cols = lax.dynamic_slice_in_dim(za_ext[slab : 2 * slab], chan_idx * block, block, 2)
    joined = jnp.concatenate([za_cols.astype(jnp.float32), coupled], axis=1)
    mixed = jnp.einsum("oc,rcw->row", unmix, joined, precision=lax.Precision.HIGHEST)
    mixed = mixed.reshape(slab, groups, mine, block).transpose(1, 0, 2, 3)
    mixed = swap(mixed, "chan", 2)
    mixed = mixed.transpose(1, 2, 0, 3).reshape(slab * mine, width)

    packed = dot3(mixed, table, 0)
    outgoing = packed.reshape(slab, chan_groups, triple, freq_groups, lanes)
    outgoing = outgoing.transpose(3, 1, 2, 0, 4).reshape(rows, triple, slab * lanes)
    got = swap(outgoing, "rows", 3)
    data = got.reshape(rows, triple, slab, lanes).transpose(2, 0, 1, 3)
    data = data.reshape(height, triple, lanes)

    freq_idx = row_idx // chan_groups
    chan_first = chan_idx * mine + row_idx % chan_groups * triple

    def own_lanes(values):
        return lax.dynamic_slice_in_dim(jnp.asarray(values), freq_idx * lanes, lanes, 0)

    sign_own = own_lanes(sign)
    other = jnp.concatenate([data[..., lanes // 2 :], data[..., : lanes // 2]], axis=2)
    pair = jnp.concatenate([data, other * sign_own], axis=2).reshape(height, triple * 2 * lanes)
    order = (np.arange(rows)[None, :] * slab + np.arange(slab)[:, None]).reshape(-1)
    angles = np.arange(height)[:, None] * order[None, :] % height * (full_turn / height)
    cosine = np.cos(angles).astype(np.float32)
    sine = np.sin(angles).astype(np.float32)
    both = jnp.dot(
        jnp.asarray(np.concatenate([cosine, sine], axis=0)), pair, precision=lax.Precision.HIGH
    ).reshape(2, height, triple, 2, lanes)
    real_part = both[0, :, :, 0] + both[1, :, :, 1]
    imag_part = both[0, :, :, 1] - both[1, :, :, 0]

    turn = freq * (full_turn / width)
    cos_v = own_lanes(np.cos(turn).astype(np.float32))[None, None, :]
    sin_v = own_lanes(np.sin(turn).astype(np.float32))[None, None, :]
    stencil = lax.dynamic_slice_in_dim(kern, chan_first, triple, 2)[..., None]
    near_real = stencil[:, 1] + (stencil[:, 0] + stencil[:, 2]) * cos_v
    near_imag = (stencil[:, 2] - stencil[:, 0]) * sin_v
    row_turn = np.arange(height) * (full_turn / height)
    cos_u = jnp.asarray(np.cos(row_turn).astype(np.float32))[:, None, None]
    sin_u = jnp.asarray(np.sin(row_turn).astype(np.float32))[:, None, None]
    symbol_real = (
        near_real[1] + (near_real[0] + near_real[2]) * cos_u + (near_imag[0] - near_imag[2]) * sin_u
    )
    symbol_imag = (
        near_imag[1] + (near_imag[0] + near_imag[2]) * cos_u + (near_real[2] - near_real[0]) * sin_u
    )
    scale = own_lanes(weight) * (1.0 / (height * width))
    factor = scale / (symbol_real * symbol_real + symbol_imag * symbol_imag)
    solved_real = (real_part * symbol_real + imag_part * symbol_imag) * factor
    solved_imag = (imag_part * symbol_real - real_part * symbol_imag) * factor
    solved = jnp.concatenate([solved_real, solved_imag], axis=0).reshape(2 * height, triple * lanes)
    back_table = np.concatenate([cosine.T, -sine.T], axis=1)
    rows_back = jnp.dot(jnp.asarray(back_table), solved, precision=lax.Precision.HIGH)
    rows_back = rows_back.reshape(slab, rows, triple, lanes).transpose(1, 2, 0, 3)
    rows_back = swap(rows_back.reshape(rows, triple, slab * lanes), "rows", 4)
    final = rows_back.reshape(freq_groups, chan_groups, triple, slab, lanes)
    final = final.transpose(3, 1, 2, 0, 4).reshape(slab * mine, width)
    return dot3(final, table, 1).reshape(slab, mine, width)


def solution(mesh):
    placed = (
        P("rows", "chan", None),
        P("rows", "chan", None),
        P(None, None, None, "chan"),
        P("chan"),
        P(None, None, "chan", None, None),
        P(),
        P(),
        P(),
    )
    return jax.shard_map(
        on_device, mesh=mesh, in_specs=placed, out_specs=P("rows", "chan", None), check_vma=False
    )
```

time: 305 us -> 144 us (0.47)
  Pallas kernels: 0 us -> 104 us
  waiting for transfers between devices: 91.8 us -> 0 us
  matrix products: 88.9 us -> 12.2 us
  starting transfers between devices: 43.1 us -> 0 us
  blocking collectives: 40.4 us -> 0 us
  between operations: 14.4 us -> 0.72 us
    pallas_call x0 -> x5, Pallas kernels: none -> 104 us  [the longest x4 73.6 us: swap(): pl.pallas_call(kernel, out_shape=jax.ShapeDtypeStruct(x.shape, x.dtype),...]
    dot_general x26 -> x8, matrix products: 86.6 us -> 9.14 us  [the longest x4 4.73 us: dot(): lax.dot_general(a, b, (((1,), (contract,)), ((), ())), preferred_element_...]
    all_to_all x3 -> x0, waiting for transfers between devices: 40.1 us -> none  [the longest x1 18.5 us: on_device(): lax.all_to_all(jnp.stack([real_part, imag_part]), 'rows', split_axis=3, c...]
    unnamed x2 -> x0, waiting for transfers between devices: 35.1 us -> none
    all_to_all x1 -> x0, blocking collectives: 28.9 us -> none  [on_device(): lax.all_to_all(solved, 'rows', split_axis=1, concat_axis=3, tiled=True)]
    all_to_all x3 -> x0, starting transfers between devices: 24.5 us -> none  [the longest x1 15.9 us: on_device(): lax.all_to_all(jnp.stack([real_part, imag_part]), 'rows', split_axis=3, c...]
    ppermute x4 -> x0, starting transfers between devices: 18.5 us -> none  [the longest x2 14.5 us: extended(): lax.ppermute(lax.slice_in_dim(block, block.shape[dim] - width, None, axis...]
    ppermute x4 -> x0, waiting for transfers between devices: 16.7 us -> none  [the longest x2 13.5 us: extended(): lax.ppermute(lax.slice_in_dim(block, 0, width, axis=dim), axis, backward)]
  transfers between devices with their start and end apart: 8 -> 0, of which waited for: 7 -> 0; matrix products, arithmetic and copies ran while one was open for 0% -> 0% of each run, Pallas kernels for 0% -> 0%
where the time goes in v1:
time: 144 us; the launch traced here: 142 us
  Pallas kernels  104 us (72%)
  local copies, waits for them, and re-layouts  20.8 us (14%)
  matrix products  12.2 us (8%)
  other arithmetic  4.39 us (3%)
    pallas_call x4, Pallas kernels, swap(): pl.pallas_call(kernel, out_shape=jax.ShapeDtypeStruct(x.shape, x.dtype),...  73.6 us
    pallas_call x1, Pallas kernels, gather(): pl.pallas_call(kernel, out_shape=(jax.ShapeDtypeStruct((3, chans) + za.sh...  30.6 us
    unnamed x55, local copies, waits for them, and re-layouts  4.97 us
    dot_general x4, matrix products, dot(): lax.dot_general(a, b, (((1,), (contract,)), ((), ())), preferred_element_...  4.73 us
    dot_general x2, matrix products, conv_rows(): jnp.einsum('rkcw,kco->row', stacked, taps, preferred_element_type=jnp.flo...  3.07 us

profile of v1, /device:TPU:1, one launch (start us, length us, event | category | flops | bytes accessed | tf_op | source)
XLA Modules:
  0.0 142.3 jit_solution(18175394926657296240)
XLA Ops:
  0.0 0.9 reshape.172
  0.9 0.6 copy.120
  1.5 1.4 %copy.62.refs_0_ = bf16[2,12,1024]{2,1,0:T(8,128)(2,1)} copy(bf16[2,12,1024]{2,0,1:T(2,128)(2,1)} %param.20) | data formatting | bytes 98304 | tf_op args[0]
  3.0 30.6 %gather_latents.1 = (bf16[3,4,2,12,1024]{4,3,2,1,0:T(8,128)(2,1)}, bf16[4,2,12,256]{3,2,1,0:T(8,128)(2,1)}) custom-call(bf16[2,12,1024]{2,1,0:T(8,128)(2,1)} %copy.62.refs_0_, bf16[4,2,12,256]{3,2,1,0:T(8,128)(2,1)} %bitcast.235), custom_call_target="tpu_custom_call" | custom-call | tf_op jit(solution)/shard_map/gather_latents/pallas_call | solution.py:134
  33.5 1.2 copy.63
  36.3 1.5 %fusion.4 = bf16[4,128,1024]{1,2,0:T(8,128)(2,1)S(1)} fusion(bf16[4,9,48,1024]{3,2,1,0:T(8,128)(2,1)S(1)} %fusion.21, bf16[9,48,128,1]{2,1,0,3:T(8,128)(2,1)S(1)} %bitcast.237, f32[128]{0:T(128)S(1)} %copy-done.15, pred[4]{0:T(512)(128)(4,1)S(1)} %slice.136), kind=kOutput, calls=%fused_computation.8 | convolution fusion | flops 455081984 | bytes 4698628 | tf_op jit(solution)/shard_map/rkcw,kco->row/dot_general | solution.py:163
  39.1 1.5 %fusion.5 = bf16[2,1024,96]{1,2,0:T(8,128)(2,1)S(1)} fusion(bf16[2,9,128,1024]{2,3,0,1:T(8,128)(2,1)S(1)} %bitcast_dynamic-update-slice_fusion, bf16[9,128,96,1]{1,2,3,0:T(8,128)(2,1)S(1)} %bitcast.212), kind=kOutput, calls=%fused_computation.10 | convolution fusion | flops 453181440 | bytes 5332992 | tf_op jit(solution)/shard_map/rkcw,kco->row/dot_general | solution.py:163
  40.8 0.8 copy.115
  41.5 9.0 %swap_chan1.1 = bf16[4,2,96,256]{3,2,1,0:T(8,128)(2,1)} custom-call(bf16[4,2,96,256]{3,2,1,0:T(8,128)(2,1)} %bitcast.220), custom_call_target="tpu_custom_call" | custom-call | tf_op jit(solution)/shard_map/swap_chan1/pallas_call | solution.py:67
  50.6 1.1 convert_reduce_fusion
  52.4 0.7 copy.119
  53.1 8.7 %swap_chan2.1 = f32[4,2,24,256]{3,2,1,0:T(8,128)} custom-call(f32[4,2,24,256]{3,2,1,0:T(8,128)} %bitcast.230), custom_call_target="tpu_custom_call" | custom-call | tf_op jit(solution)/shard_map/swap_chan2/pallas_call | solution.py:67
  61.7 1.1 copy.77
  62.9 1.2 reduce-precision_convert_fusion
  64.1 1.3 copy-done.1
  65.4 0.5 fusion.31
  66.0 0.5 convolution_add_fusion.2
  67.2 0.8 copy.80.refs_0_
  68.0 34.0 %swap_rows3.1 = f32[128,3,128]{2,1,0:T(4,128)} custom-call(f32[128,3,128]{2,1,0:T(4,128)} %copy.80.refs_0_), custom_call_target="tpu_custom_call" | custom-call | tf_op jit(solution)/shard_map/swap_rows3/pallas_call | solution.py:67
  102.0 1.1 copy.81
  103.2 0.8 dynamic_slice.19
  104.1 2.5 %fusion.52 = f32[512,384]{0,1:T(8,128)} fusion(f32[512,256]{1,0:T(8,128)} %constant.91.clone, f32[256,384]{0,1:T(8,128)S(1)} %bitcast.223), kind=kOutput, calls=%fused_computation.124 | convolution fusion | flops 301989888 | bytes 1703936 | tf_op jit(solution)/shard_map/dot_general | solution.py:265
  106.6 1.6 %reshape.183 = f32[2,256,3,2,64]{1,0,4,3,2:T(2,128)S(1)} reshape(f32[512,384]{0,1:T(8,128)} %fusion.52) | data formatting | bytes 1572864 | tf_op jit(solution)/shard_map/reshape | solution.py:267
  108.8 0.8 dynamic_slice.21
  109.9 0.8 dynamic_slice.22
  111.0 0.8 dynamic-slice_multiply_fusion
  112.1 1.3 fusion.53
  113.9 0.8 copy.85.refs_0_
  114.7 21.9 %swap_rows4.1 = f32[128,3,128]{2,1,0:T(4,128)} custom-call(f32[128,3,128]{2,1,0:T(4,128)} %copy.85.refs_0_), custom_call_target="tpu_custom_call" | custom-call | tf_op jit(solution)/shard_map/swap_rows4/pallas_call | solution.py:67
  136.6 1.2 reshape.195
  138.1 2.4 %fusion.35 = f32[96,1024]{1,0:T(8,128)S(1)} fusion(bf16[1024,1024]{1,0:T(8,128)(2,1)} %bitcast.216, bf16[48,1024]{1,0:T(8,128)(2,1)S(1)} %get-tuple-element.24, bf16[48,1024]{1,0:T(8,128)(2,1)S(1)} %get-tuple-element.23), kind=kOutput, calls=%fused_computation.78 | convolution fusion | flops 201719808 | bytes 2686976 | tf_op jit(solution)/shard_map/dot_general | solution.py:196
  140.8 1.4 %convolution_add_fusion = f32[48,1024]{1,0:T(8,128)} fusion(bf16[48,1024]{1,0:T(8,128)(2,1)S(1)} %convert_element_type.95, bf16[1024,1024]{1,0:T(8,128)(2,1)S(1)} %bitcast.214, f32[96,1024]{1,0:T(8,128)S(1)} %fusion.35), kind=kOutput, calls=%fused_computation.11 | convolution fusion | flops 100761600 | bytes 2785280 | tf_op jit(solution)/shard_map/dot_general | solution.py:196
  (101 shorter events, 7.0 us)
Async XLA Ops:
  0.0 39.1 %copy-start = (bf16[3,3,128,2,48]{2,4,3,1,0:T(8,128)(2,1)S(1)}, bf16[3,3,128,2,48]{2,4,3,1,0:T(8,128)(2,1)}, u32[]{:S(2)}) copy-start(bf16[3,3,128,2,48]{2,4,3,1,0:T(8,128)(2,1)} %param.24) | copy-start | bytes 663556
  35.2 1.1 copy-start.13
  35.2 1.1 copy-start.15
  39.1 12.5 %copy-start.14 = (f32[2,48]{1,0:T(2,128)S(1)}, f32[2,48]{1,0:T(2,128)}, u32[]{:S(2)}) copy-start(f32[2,48]{1,0:T(2,128)} %param.25) | copy-start | bytes 1156
  39.1 12.7 %copy-start.8 = (bf16[4,2,12,256]{3,2,1,0:T(8,128)(2,1)S(1)}, bf16[4,2,12,256]{3,2,1,0:T(8,128)(2,1)}, u32[]{:S(2)}) copy-start(bf16[4,2,12,256]{3,2,1,0:T(8,128)(2,1)} %get-tuple-element.12) | copy-start | bytes 147460
  39.1 12.9 %copy-start.9 = (f32[96,96]{1,0:T(8,128)S(1)}, f32[96,96]{1,0:T(8,128)}, u32[]{:S(2)}) copy-start(f32[96,96]{1,0:T(8,128)} %param.26) | copy-start | bytes 110596
  40.7 22.2 %copy-start.4 = (f32[32,1024]{1,0:T(8,128)S(1)}, f32[32,1024]{1,0:T(8,128)}, u32[]{:S(2)}) copy-start(f32[32,1024]{1,0:T(8,128)} %constant.86.clone) | copy-start | bytes 393220
  40.7 22.2 %copy-start.5 = (f32[32,1024]{1,0:T(8,128)S(1)}, f32[32,1024]{1,0:T(8,128)}, u32[]{:S(2)}) copy-start(f32[32,1024]{1,0:T(8,128)} %constant.87.clone) | copy-start | bytes 393220
  40.7 22.2 %copy-start.6 = (f32[32,1024]{1,0:T(8,128)S(1)}, f32[32,1024]{1,0:T(8,128)}, u32[]{:S(2)}) copy-start(f32[32,1024]{1,0:T(8,128)} %constant.88.clone) | copy-start | bytes 393220
  40.7 22.2 %copy-start.7 = (f32[32,1024]{1,0:T(8,128)S(1)}, f32[32,1024]{1,0:T(8,128)}, u32[]{:S(2)}) copy-start(f32[32,1024]{1,0:T(8,128)} %constant.89.clone) | copy-start | bytes 393220
  62.9 3.0 %copy-start.2 = (f32[4,2,24,256]{3,2,1,0:T(8,128)S(1)}, f32[4,2,24,256]{3,2,1,0:T(8,128)}, u32[]{:S(2)}) copy-start(f32[4,2,24,256]{3,2,1,0:T(8,128)} %swap_chan2.1) | copy-start | bytes 589828
  64.1 1.3 copy-start.1
  103.1 5.6 %copy-start.10 = (f32[3,3,96]{2,1,0:T(4,128)S(1)}, f32[3,3,96]{2,1,0:T(4,128)}, u32[]{:S(2)}) copy-start(f32[3,3,96]{2,1,0:T(4,128)} %param.27) | copy-start | bytes 10372
  103.1 8.7 %copy-start.11 = (f32[256]{0:T(256)S(1)}, f32[256]{0:T(256)}, u32[]{:S(2)}) copy-start(f32[256]{0:T(256)} %constant.94.clone) | copy-start | bytes 3076
  103.1 8.7 %copy-start.12 = (f32[256]{0:T(256)S(1)}, f32[256]{0:T(256)}, u32[]{:S(2)}) copy-start(f32[256]{0:T(256)} %constant.95.clone) | copy-start | bytes 3076
  104.1 9.3 %copy-start.3 = (f32[256,256]{1,0:T(8,128)S(1)}, f32[256,256]{1,0:T(8,128)}, u32[]{:S(2)}) copy-start(f32[256,256]{1,0:T(8,128)} %constant.105) | copy-start | bytes 786436

commit v2 on v1

--- a/solution.py
+++ b/solution.py
@@ -79,88 +79,152 @@
     )(x)
 
 
-def gather_kernel(rows, chans, za_ref, zb_ref, out_ref, zb_out, sems_a, sems_b, own_sem):
+def gather_kernel(rows, chans, halves_of, *refs):
+    za_ref, zb_ref, win_ref, wout_ref, bias_ref = refs[:5]
+    za_out, zb_out, win_out, wout_out, bias_out = refs[5:10]
+    za_sems, zb_sems, w_sems, pass_sems, own_sem = refs[10:]
     me_row = lax.axis_index("rows")
     me_chan = lax.axis_index("chan")
+    core = lax.rem(me_row, 2)
+    side = lax.rem(me_row // 2, halves_of)
+    ring = halves_of * chans
+    spot = side * chans + me_chan
+    partner = (me_row + 1 - 2 * core, me_chan)
     barrier = pltpu.get_barrier_semaphore()
     peers = [(dr, dc) for dr in (0, 1, 2) for dc in range(chans) if (dr, dc) != (1, 0)]
+    steps = (1, ring - 1, 2 + core * (ring - 4))
 
     def place(dr, dc):
         return (lax.rem(me_row + dr + rows - 1, rows), lax.rem(me_chan + dc, chans))
 
+    def around(step):
+        there = lax.rem(spot + step, ring)
+        return (me_row + (there // chans - side) * 2, lax.rem(there, chans))
+
+    for step in steps:
+        pl.semaphore_signal(
+            barrier, inc=1, device_id=around(ring - step), device_id_type=mesh_ids
+        )
     for dr, dc in peers:
         pl.semaphore_signal(barrier, inc=1, device_id=place(dr, dc), device_id_type=mesh_ids)
-    own = pltpu.make_async_copy(za_ref, out_ref.at[1, me_chan], own_sem.at[0])
-    own.start()
-    own_b = pltpu.make_async_copy(zb_ref.at[me_chan], zb_out.at[me_chan], own_sem.at[1])
-    own_b.start()
-    pl.semaphore_wait(barrier, len(peers))
+    own = [
+        pltpu.make_async_copy(win_ref, win_out.at[me_chan], own_sem.at[0]),
+        pltpu.make_async_copy(wout_ref, wout_out.at[me_chan], own_sem.at[1]),
+        pltpu.make_async_copy(za_ref.at[me_chan], za_out.at[1, me_chan], own_sem.at[2]),
+        pltpu.make_async_copy(zb_ref.at[me_chan], zb_out.at[me_chan], own_sem.at[3]),
+        pltpu.make_async_copy(bias_ref, bias_out.at[me_chan], own_sem.at[4]),
+    ]
+    for one in own:
+        one.start()
+    pl.semaphore_wait(barrier, len(peers) + len(steps))
+    first = []
+    for idx, step in enumerate(steps):
+        for kind, (source, target) in enumerate(((wout_ref, wout_out), (win_ref, win_out))):
+            first.append(
+                pltpu.make_async_remote_copy(
+                    src_ref=source.at[core],
+                    dst_ref=target.at[me_chan, core],
+                    send_sem=w_sems.at[0, kind, idx],
+                    recv_sem=w_sems.at[1, kind, idx],
+                    device_id=around(step),
+                    device_id_type=mesh_ids,
+                )
+            )
     copies = []
     for idx, (dr, dc) in enumerate(peers):
+        there = place(dr, dc)
         copies.append(
             pltpu.make_async_remote_copy(
-                src_ref=za_ref,
-                dst_ref=out_ref.at[2 - dr, me_chan],
-                send_sem=sems_a.at[0, idx],
-                recv_sem=sems_a.at[1, idx],
-                device_id=place(dr, dc),
+                src_ref=za_ref.at[there[1]],
+                dst_ref=za_out.at[2 - dr, me_chan],
+                send_sem=za_sems.at[0, idx],
+                recv_sem=za_sems.at[1, idx],
+                device_id=there,
                 device_id_type=mesh_ids,
             )
         )
     for dc in range(1, chans):
         peer = lax.rem(me_chan + dc, chans)
-        copies.append(
-            pltpu.make_async_remote_copy(
-                src_ref=zb_ref.at[peer],
-                dst_ref=zb_out.at[me_chan],
-                send_sem=sems_b.at[0, dc],
-                recv_sem=sems_b.at[1, dc],
-                device_id=(me_row, peer),
+        pairs = ((zb_ref.at[peer], zb_out), (bias_ref, bias_out))
+        for kind, (source, target) in enumerate(pairs):
+            copies.append(
+                pltpu.make_async_remote_copy(
+                    src_ref=source,
+                    dst_ref=target.at[me_chan],
+                    send_sem=zb_sems.at[0, kind, dc],
+                    recv_sem=zb_sems.at[1, kind, dc],
+                    device_id=(me_row, peer),
+                    device_id_type=mesh_ids,
+                )
+            )
+    for one in first:
+        one.start()
+    for one in copies:
+        one.start()
+    passed = []
+    for idx, step in enumerate(steps):
+        origin = lax.rem(spot + ring - step, ring)
+        quarter = lax.rem(origin, chans)
+        for kind, target in enumerate((wout_out, win_out)):
+            first[2 * idx + kind].wait_recv()
+            one = pltpu.make_async_remote_copy(
+                src_ref=target.at[quarter, core],
+                dst_ref=target.at[quarter, core],
+                send_sem=pass_sems.at[0, kind, idx],
+                recv_sem=pass_sems.at[1, kind, idx],
+                device_id=partner,
                 device_id_type=mesh_ids,
             )
-        )
-    for one in copies:
-        one.start()
-    own.wait()
-    own_b.wait()
+            one.start()
+            passed.append(one)
+    for one in own:
+        one.wait()
     for one in copies:
         one.wait()
-
-
-def gather(za, zb_cols, rows, chans):
+    for one in passed:
+        one.wait()
+    for one in first:
+        one.wait_send()
+
+
+def gather(za_cols, zb_cols, w_in, w_out, bias, rows, chans, halves_of):
     def kernel(*refs):
-        gather_kernel(rows, chans, *refs)
+        gather_kernel(rows, chans, halves_of, *refs)
+
+    def several(lead, x):
+        return jax.ShapeDtypeStruct(lead + x.shape, x.dtype)
 
     return pl.pallas_call(
         kernel,
         out_shape=(
-            jax.ShapeDtypeStruct((3, chans) + za.shape, za.dtype),
-            jax.ShapeDtypeStruct(zb_cols.shape, zb_cols.dtype),
+            several((3,), za_cols),
+            several((), zb_cols),
+            several((chans,), w_in),
+            several((chans,), w_out),
+            several((chans,), bias),
         ),
-        in_specs=[vmem, vmem],
-        out_specs=(vmem, vmem),
+        in_specs=[vmem] * 5,
+        out_specs=(vmem,) * 5,
         scratch_shapes=[
             pltpu.SemaphoreType.DMA((2, 3 * chans)),
-            pltpu.SemaphoreType.DMA((2, chans)),
-            pltpu.SemaphoreType.DMA((2,)),
+            pltpu.SemaphoreType.DMA((2, 2, chans)),
+            pltpu.SemaphoreType.DMA((2, 2, 3)),
+            pltpu.SemaphoreType.DMA((2, 2, 3)),
+            pltpu.SemaphoreType.DMA((5,)),
         ],
         compiler_params=pltpu.CompilerParams(collective_id=0, has_side_effects=True),
-        name="gather_latents",
-    )(za, zb_cols)
-
-
-def conv_rows(source, weight):
+        name="gather_inputs",
+    )(za_cols, zb_cols, w_in, w_out, bias)
+
+
+def taps_of(source, width):
     rows_out = source.shape[0] - 2
-    width = source.shape[2]
-    padded = jnp.pad(source, ((0, 0), (0, 0), (1, 1)))
     pieces = [
-        padded[row_off : row_off + rows_out, :, col_off : col_off + width]
+        source[row_off : row_off + rows_out, :, col_off : col_off + width]
         for row_off in range(3)
         for col_off in range(3)
     ]
-    stacked = jnp.stack(pieces, axis=1)
-    taps = weight.reshape(9, weight.shape[2], weight.shape[3])
-    return jnp.einsum("rkcw,kco->row", stacked, taps, preferred_element_type=jnp.float32)
+    return jnp.stack(pieces, axis=1)
 
 
 def halves(values):
@@ -220,26 +284,52 @@
 
     table, freq, sign, weight = column_tables(width, lanes // 2)
 
-    zb_cols = zb.reshape(slab, quarter, groups, block).transpose(2, 0, 1, 3)
-    za_got, zb_got = gather(za, zb_cols, rows, groups)
-    za_ext = za_got.transpose(0, 2, 1, 3, 4).reshape(3 * slab, half, width)
+    zb_cols = zb.reshape(slab * quarter, groups, block).transpose(1, 0, 2)
+    za_wide = jnp.pad(za.reshape(slab * quarter, width), ((0, 0), (2, 128 + 2)))
+    za_cols = jnp.stack(
+        [za_wide[:, block * i : block * i + block + 128] for i in range(groups)], axis=0
+    )
+    taps = 9
+    w_in_parts = w_in.reshape(2, taps * half // 2, hidden_local)
+    w_out_parts = w_out.reshape(taps * hidden_local, chans).T.reshape(
+        2, chans // 2, taps * hidden_local
+    )
+    za_got, zb_got, w_in_all, w_out_all, bias = gather(
+        za_cols, zb_cols, w_in_parts, w_out_parts, b_in[None, :], rows, groups, 2
+    )
+    za_ext = za_got.reshape(3, groups, slab, quarter, block + 128)[..., : block + 4]
+    za_ext = za_ext.transpose(0, 2, 1, 3, 4).reshape(3 * slab, half, block + 4)
     ext_rows = row_idx * slab - slab + jnp.arange(3 * slab, dtype=jnp.int32)
     inside = (ext_rows >= 0) & (ext_rows < height)
     za_ext = jnp.where(inside[:, None, None], za_ext, jnp.zeros((), za.dtype))
-    hidden = jax.nn.relu(conv_rows(za_ext, w_in) + b_in[None, :, None])
-    hidden = jnp.where(inside[1:-1][:, None, None], hidden, 0.0).astype(jnp.bfloat16)
-    w_flat = w_out.reshape(3, 3, hidden_local, chans)
-    share = conv_rows(hidden, w_flat).astype(jnp.bfloat16)
-    share = share.reshape(slab, chans, groups, block).transpose(2, 0, 1, 3)
-    raw = jnp.sum(swap(share, "chan", 1).astype(jnp.float32), axis=0)
+    ext_cols = chan_idx * block - 1 + jnp.arange(block + 2, dtype=jnp.int32)
+    inside_cols = (ext_cols >= 0) & (ext_cols < width)
+    hidden_units = groups * hidden_local
+    hidden = jnp.einsum(
+        "rkcw,qkco->rqow",
+        taps_of(za_ext, block + 2),
+        w_in_all.reshape(groups, taps, half, hidden_local),
+        preferred_element_type=jnp.float32,
+    ).reshape(2 * slab, hidden_units, block + 2)
+    hidden = jax.nn.relu(hidden + bias.reshape(hidden_units)[None, :, None])
+    keep = inside[1:-1][:, None, None] & inside_cols[None, None, :]
+    hidden = jnp.where(keep, hidden, 0.0).astype(jnp.bfloat16)
+    hidden_taps = taps_of(hidden, block).reshape(slab, taps, groups, hidden_local, block)
+    raw = jnp.einsum(
+        "rkqcw,qokc->row",
+        hidden_taps,
+        w_out_all.reshape(groups, chans, taps, hidden_local),
+        preferred_element_type=jnp.float32,
+    )
     raw = raw + b_out.reshape(chans)[None, :, None]
-    latent = zb_got.transpose(1, 0, 2, 3).reshape(slab, half, block).astype(jnp.float32)
+    latent = zb_got.reshape(groups, slab, quarter, block).transpose(1, 0, 2, 3)
+    latent = latent.reshape(slab, half, block).astype(jnp.float32)
     coupled = (latent - raw[:, half:]) * jnp.exp(-jnp.tanh(raw[:, :half]))
-    za_cols = lax.dynamic_slice_in_dim(za_ext[slab : 2 * slab], chan_idx * block, block, 2)
-    joined = jnp.concatenate([za_cols.astype(jnp.float32), coupled], axis=1)
+    za_own = za_ext[slab : 2 * slab, :, 2 : 2 + block]
+    joined = jnp.concatenate([za_own.astype(jnp.float32), coupled], axis=1)
     mixed = jnp.einsum("oc,rcw->row", unmix, joined, precision=lax.Precision.HIGHEST)
     mixed = mixed.reshape(slab, groups, mine, block).transpose(1, 0, 2, 3)
-    mixed = swap(mixed, "chan", 2)
+    mixed = swap(mixed, "chan", 1)
     mixed = mixed.transpose(1, 2, 0, 3).reshape(slab * mine, width)
 
     packed = dot3(mixed, table, 0)
@@ -253,7 +343,8 @@
     chan_first = chan_idx * mine + row_idx % chan_groups * triple
 
     def own_lanes(values):
-        return lax.dynamic_slice_in_dim(jnp.asarray(values), freq_idx * lanes, lanes, 0)
+        grouped = jnp.asarray(values).reshape(freq_groups, lanes)
+        return lax.dynamic_index_in_dim(grouped, freq_idx, 0, keepdims=False)
 
     sign_own = own_lanes(sign)
     other = jnp.concatenate([data[..., lanes // 2 :], data[..., : lanes // 2]], axis=2)

time: 144 us -> 151 us (1.049)
  local copies, waits for them, and re-layouts: 20.8 us -> 45.1 us
  Pallas kernels: 104 us -> 88.9 us
    pallas_call x4 -> x3, Pallas kernels: 73.6 us -> 61.8 us  [swap(): pl.pallas_call(kernel, out_shape=jax.ShapeDtypeStruct(x.shape, x.dtype),...]
    unnamed x55 -> x61, local copies, waits for them, and re-layouts: 4.97 us -> 15.8 us
    slice x2 -> x11, local copies, waits for them, and re-layouts: 0.09 us -> 9.85 us  [the longest x10 9.77 us: taps_of(): source[row_off:row_off + rows_out, :, col_off:col_off + width]]
    pallas_call x1, Pallas kernels: 30.6 us -> 27 us  [gather(): pl.pallas_call(kernel, out_shape=(several((3,), za_cols), several((), zb_...]
    dynamic_slice x3 -> x0, local copies, waits for them, and re-layouts: 2.29 us -> none  [own_lanes(): lax.dynamic_slice_in_dim(jnp.asarray(values), freq_idx * lanes, lanes, 0)]
    reshape x4 -> x7, local copies, waits for them, and re-layouts: 2.43 us -> 4.25 us  [the longest x1 2.1 us: on_device(): hidden = jnp.einsum('rkcw,qkco->rqow', taps_of(za_ext, block + 2), w_in_a...]
    transpose x1 -> x3, local copies, waits for them, and re-layouts: 1.2 us -> 2.84 us  [the longest x1 2.72 us: on_device(): jnp.einsum('rkcw,qkco->rqow', taps_of(za_ext, block + 2), w_in_all.reshap...]
where the time goes in v2:
time: 151 us; the launch traced here: 150 us
  Pallas kernels  88.9 us (59%)
  local copies, waits for them, and re-layouts  45.1 us (30%)
  matrix products  11.1 us (7%)
  other arithmetic  4.32 us (3%)
    pallas_call x3, Pallas kernels, swap(): pl.pallas_call(kernel, out_shape=jax.ShapeDtypeStruct(x.shape, x.dtype),...  61.8 us
    pallas_call x1, Pallas kernels, gather(): pl.pallas_call(kernel, out_shape=(several((3,), za_cols), several((), zb_...  27 us
    unnamed x61, local copies, waits for them, and re-layouts  15.8 us
    slice x10, local copies, waits for them, and re-layouts, taps_of(): source[row_off:row_off + rows_out, :, col_off:col_off + width]  9.77 us
    dot_general x4, matrix products, dot(): lax.dot_general(a, b, (((1,), (contract,)), ((), ())), preferred_element_...  4.73 us
    dot_general x1, matrix products, on_device(): jnp.einsum('rkqcw,qokc->row', hidden_taps, w_out_all.reshape(groups, chan...  3.12 us

profile of v2, /device:TPU:1, one launch (start us, length us, event | category | flops | bytes accessed | tf_op | source)
XLA Modules:
  0.0 150.0 jit_solution(2867141511398066255)
XLA Ops:
  1.6 1.1 copy.79
  2.7 0.9 reshape.271
  5.0 27.0 %gather_inputs.1 = (bf16[3,4,24,384]{3,2,1,0:T(8,128)(2,1)}, bf16[4,24,256]{2,1,0:T(8,128)(2,1)}, bf16[4,2,216,128]{3,2,1,0:T(8,128)(2,1)}, bf16[4,2,48,1152]{3,2,1,0:T(8,128)(2,1)}, f32[4,1,128]{2,1,0:T(1,128)}) custom-call(bf16[4,24,384]{2,1,0:T(8,128)(2,1)} %pad_maximum_fusion.1.refs_0_, bf16[4,24,256]{2,1,0:T(8,128)(2,1)} %bitcast.249, ...), custom_call_target="tpu_custom_call" | custom-call | tf_op jit(solution)/shard_map/gather_inputs/pallas_call | solution.py:197
  32.1 1.0 copy.80
  35.1 2.7 %copy.92 = f32[4,4,128,258]{2,1,3,0:T(4,128)} copy(f32[4,4,128,258]{2,3,0,1:T(8,128)S(1)} %convolution_bitcast_fusion) | data formatting | bytes 4227072 | tf_op jit(solution)/shard_map/rkcw,qkco->rqow/transpose | solution.py:308
  37.9 2.1 %reshape.277 = f32[4,512,258]{1,2,0:T(8,128)S(1)} reshape(f32[4,4,128,258]{2,1,3,0:T(4,128)} %copy.92) | data formatting | bytes 4227072 | tf_op jit(solution)/shard_map/reshape | solution.py:313
  40.5 1.6 %fusion.51 = (bf16[2,512,256]{1,2,0:T(8,128)(2,1)S(1)}, bf16[2,512,256]{1,2,0:T(8,128)(2,1)S(1)}, bf16[2,512,256]{1,2,0:T(8,128)(2,1)S(1)}, bf16[2,512,256]{1,2,...) fusion(bf16[4,512,258]{1,2,0:T(8,128)(2,1)S(1)} %select_convert, ...), kind=kLoop, calls=%fused_computation.131 | loop fusion | bytes 9437184 | tf_op jit(solution)/shard_map/slice | solution.py:223
  42.1 2.0 %copy.93 = bf16[2,512,256]{2,1,0:T(8,128)(2,1)} copy(bf16[2,512,256]{1,2,0:T(8,128)(2,1)} %get-tuple-element.31) | data formatting | bytes 1048576 | tf_op jit(solution)/shard_map/slice | solution.py:223
  44.2 1.9 %constant_dynamic-update-slice_fusion.8 = bf16[2,9,4,128,256]{4,3,2,1,0:T(8,128)(2,1)} fusion(bf16[2,1,4,128,256]{4,3,2,1,0:T(8,128)(2,1)} %bitcast.229), kind=kLoop, calls=%fused_computation.96 | loop fusion | bytes 1048576
  46.1 2.0 %copy.94 = bf16[2,512,256]{2,1,0:T(8,128)(2,1)} copy(bf16[2,512,256]{1,2,0:T(8,128)(2,1)} %get-tuple-element.30) | data formatting | bytes 1048576 | tf_op jit(solution)/shard_map/slice | solution.py:223
  48.1 1.9 %constant_dynamic-update-slice_fusion.7 = bf16[2,9,4,128,256]{4,3,2,1,0:T(8,128)(2,1)} fusion(bf16[2,9,4,128,256]{4,3,2,1,0:T(8,128)(2,1)} %constant_dynamic-update-slice_fusion.8, bf16[2,1,4,128,256]{4,3,2,1,0:T(8,128)(2,1)} %bitcast.221), kind=kLoop, calls=%fused_computation.95 | loop fusion | bytes 1048576
  50.0 2.0 %copy.95 = bf16[2,512,256]{2,1,0:T(8,128)(2,1)} copy(bf16[2,512,256]{1,2,0:T(8,128)(2,1)} %get-tuple-element.29) | data formatting | bytes 1048576 | tf_op jit(solution)/shard_map/slice | solution.py:223
  52.0 1.9 %constant_dynamic-update-slice_fusion.6 = bf16[2,9,4,128,256]{4,3,2,1,0:T(8,128)(2,1)} fusion(bf16[2,9,4,128,256]{4,3,2,1,0:T(8,128)(2,1)} %constant_dynamic-update-slice_fusion.7, bf16[2,1,4,128,256]{4,3,2,1,0:T(8,128)(2,1)} %bitcast.222), kind=kLoop, calls=%fused_computation.94 | loop fusion | bytes 1048576
  53.9 1.0 copy.96
  54.9 1.9 %constant_dynamic-update-slice_fusion.5 = bf16[2,9,4,128,256]{4,3,2,1,0:T(8,128)(2,1)} fusion(bf16[2,9,4,128,256]{4,3,2,1,0:T(8,128)(2,1)} %constant_dynamic-update-slice_fusion.6, bf16[2,1,4,128,256]{4,3,2,1,0:T(8,128)(2,1)} %bitcast.223), kind=kLoop, calls=%fused_computation.93 | loop fusion | bytes 1048576
  57.0 0.8 constant_dynamic-update-slice_fusion.4
  59.1 0.8 constant_dynamic-update-slice_fusion.2
  62.7 3.1 %fusion.4 = f32[2,96,256]{2,1,0:T(8,128)S(1)} fusion(bf16[2,9,4,128,256]{4,3,2,1,0:T(8,128)(2,1)} %constant_dynamic-update-slice_fusion, bf16[4,96,9,128]{3,2,1,0:T(8,128)(2,1)S(1)} %reshape.275, f32[96]{0:T(128)S(1)} %add.164), kind=kOutput, calls=%fused_computation.13 | convolution fusion | flops 453033984 | bytes 5800320 | tf_op jit(solution)/shard_map/rkqcw,qokc->row/dot_general | solution.py:318
  67.2 10.7 %swap_chan1.1 = f32[4,2,24,256]{3,2,1,0:T(8,128)} custom-call(f32[4,2,24,256]{3,2,1,0:T(8,128)} %bitcast.242), custom_call_target="tpu_custom_call" | custom-call | tf_op jit(solution)/shard_map/swap_chan1/pallas_call | solution.py:67
  77.9 1.1 copy.105
  79.1 1.1 reduce-precision_convert_fusion
  80.2 1.3 copy-done.1
  83.3 0.9 copy.108.refs_0_
  84.2 28.3 %swap_rows3.1 = f32[128,3,128]{2,1,0:T(4,128)} custom-call(f32[128,3,128]{2,1,0:T(4,128)} %copy.108.refs_0_), custom_call_target="tpu_custom_call" | custom-call | tf_op jit(solution)/shard_map/swap_rows3/pallas_call | solution.py:67
  112.5 1.1 copy.109
  114.5 1.4 fusion.54
  115.9 1.7 %reshape.286 = f32[2,256,3,2,64]{1,0,4,3,2:T(2,128)S(1)} reshape(f32[512,384]{0,1:T(8,128)} %fusion.54) | data formatting | bytes 1572864 | tf_op jit(solution)/shard_map/reshape | solution.py:358
  120.7 0.8 copy.113.refs_0_
  121.5 22.8 %swap_rows4.1 = f32[128,3,128]{2,1,0:T(4,128)} custom-call(f32[128,3,128]{2,1,0:T(4,128)} %copy.113.refs_0_), custom_call_target="tpu_custom_call" | custom-call | tf_op jit(solution)/shard_map/swap_rows4/pallas_call | solution.py:67
  144.4 1.2 reshape.303
  145.9 2.4 %fusion.17 = f32[96,1024]{1,0:T(8,128)S(1)} fusion(bf16[1024,1024]{1,0:T(8,128)(2,1)} %bitcast.220, bf16[48,1024]{1,0:T(8,128)(2,1)S(1)} %get-tuple-element.39, bf16[48,1024]{1,0:T(8,128)(2,1)S(1)} %get-tuple-element.38), kind=kOutput, calls=%fused_computation.42 | convolution fusion | flops 201719808 | bytes 2686976 | tf_op jit(solution)/shard_map/dot_general | solution.py:260
  148.6 1.4 convolution_add_fusion
  (122 shorter events, 17.1 us)
Async XLA Ops:
  0.0 66.1 %copy-start = (f32[96,96]{1,0:T(8,128)S(1)}, f32[96,96]{1,0:T(8,128)}, u32[]{:S(2)}) copy-start(f32[96,96]{1,0:T(8,128)} %param.26) | copy-start | bytes 110596
  33.2 1.1 copy-start.5
  37.9 2.3 %copy-start.14 = (f32[4,1,128]{2,1,0:T(1,128)S(1)}, f32[4,1,128]{2,1,0:T(1,128)}, u32[]{:S(2)}) copy-start(f32[4,1,128]{2,1,0:T(1,128)} %get-tuple-element.18) | copy-start | bytes 6148
  60.0 2.1 %copy-start.3 = (bf16[4,2,48,1152]{3,2,1,0:T(8,128)(2,1)S(1)}, bf16[4,2,48,1152]{3,2,1,0:T(8,128)(2,1)}, u32[]{:S(2)}) copy-start(bf16[4,2,48,1152]{3,2,1,0:T(8,128)(2,1)} %get-tuple-element.16) | copy-start | bytes 2654212
  61.0 1.6 %copy-start.17 = (f32[2,48]{1,0:T(2,128)S(1)}, f32[2,48]{1,0:T(2,128)}, u32[]{:S(2)}) copy-start(f32[2,48]{1,0:T(2,128)} %param.25) | copy-start | bytes 1156
  62.7 3.2 %copy-start.12 = (bf16[4,24,256]{2,1,0:T(8,128)(2,1)S(1)}, bf16[4,24,256]{2,1,0:T(8,128)(2,1)}, u32[]{:S(2)}) copy-start(bf16[4,24,256]{2,1,0:T(8,128)(2,1)} %get-tuple-element.15) | copy-start | bytes 147460
  65.8 13.2 %copy-start.8 = (f32[32,1024]{1,0:T(8,128)S(1)}, f32[32,1024]{1,0:T(8,128)}, u32[]{:S(2)}) copy-start(f32[32,1024]{1,0:T(8,128)} %constant.100.clone) | copy-start | bytes 393220
  65.8 13.2 %copy-start.9 = (f32[32,1024]{1,0:T(8,128)S(1)}, f32[32,1024]{1,0:T(8,128)}, u32[]{:S(2)}) copy-start(f32[32,1024]{1,0:T(8,128)} %constant.101.clone) | copy-start | bytes 393220
  65.8 13.2 %copy-start.10 = (f32[32,1024]{1,0:T(8,128)S(1)}, f32[32,1024]{1,0:T(8,128)}, u32[]{:S(2)}) copy-start(f32[32,1024]{1,0:T(8,128)} %constant.98.clone) | copy-start | bytes 393220
  65.8 13.2 %copy-start.11 = (f32[32,1024]{1,0:T(8,128)S(1)}, f32[32,1024]{1,0:T(8,128)}, u32[]{:S(2)}) copy-start(f32[32,1024]{1,0:T(8,128)} %constant.99.clone) | copy-start | bytes 393220
  80.2 1.4 copy-start.1
  80.2 1.8 %copy-start.2 = (f32[4,2,24,256]{3,2,1,0:T(8,128)S(1)}, f32[4,2,24,256]{3,2,1,0:T(8,128)}, u32[]{:S(2)}) copy-start(f32[4,2,24,256]{3,2,1,0:T(8,128)} %swap_chan1.1) | copy-start | bytes 589828
  83.1 31.4 %copy-start.4 = (f32[512,256]{1,0:T(8,128)S(1)}, f32[512,256]{1,0:T(8,128)}, u32[]{:S(2)}) copy-start(f32[512,256]{1,0:T(8,128)} %constant.103.clone) | copy-start | bytes 1572868
  115.9 2.2 %copy-start.13 = (f32[3,3,96]{2,1,0:T(4,128)S(1)}, f32[3,3,96]{2,1,0:T(4,128)}, u32[]{:S(2)}) copy-start(f32[3,3,96]{2,1,0:T(4,128)} %param.27) | copy-start | bytes 10372
  115.9 3.7 %copy-start.15 = (f32[256]{0:T(256)S(1)}, f32[256]{0:T(256)}, u32[]{:S(2)}) copy-start(f32[256]{0:T(256)} %constant.106.clone) | copy-start | bytes 3076
  115.9 3.7 %copy-start.16 = (f32[256]{0:T(256)S(1)}, f32[256]{0:T(256)}, u32[]{:S(2)}) copy-start(f32[256]{0:T(256)} %constant.107.clone) | copy-start | bytes 3076
  115.9 4.0 %copy-start.7 = (f32[256,256]{1,0:T(8,128)S(1)}, f32[256,256]{1,0:T(8,128)}, u32[]{:S(2)}) copy-start(f32[256,256]{1,0:T(8,128)} %constant.118) | copy-start | bytes 786436
  117.5 2.7 %copy-start.6 = (f32[256,256]{1,0:T(8,128)S(1)}, f32[256,256]{1,0:T(8,128)}, u32[]{:S(2)}) copy-start(f32[256,256]{1,0:T(8,128)} %constant.119) | copy-start | bytes 786436

commit v3 on v2

--- a/solution.py
+++ b/solution.py
@@ -217,14 +217,79 @@
     )(za_cols, zb_cols, w_in, w_out, bias)
 
 
-def taps_of(source, width):
-    rows_out = source.shape[0] - 2
-    pieces = [
-        source[row_off : row_off + rows_out, :, col_off : col_off + width]
-        for row_off in range(3)
-        for col_off in range(3)
-    ]
-    return jnp.stack(pieces, axis=1)
+def couple_kernel(dims, *refs):
+    slab, half, quarter, hidden_local, groups, block, width, height = dims
+    za_ref, zb_ref, win_ref, wout_ref, bias_ref, bout_ref, unmix_ref, out_ref = refs[:8]
+    taps_ref, hidden_ref = refs[8:]
+    wide = za_ref.shape[2]
+    first_row = lax.axis_index("rows") * slab - slab
+    first_col = lax.axis_index("chan") * block - 1
+    span = 3 * half
+    for row in range(3 * slab):
+        plane = za_ref[row].astype(jnp.float32)
+        for off in range(3):
+            moved = plane if off == 0 else pltpu.roll(plane, wide - off, 1)
+            taps_ref[pl.ds(row * span + off * half, half), :] = moved.astype(jnp.bfloat16)
+    cols = first_col + lax.broadcasted_iota(jnp.int32, (hidden_local, wide), 1)
+    inside = (cols >= 0) & (cols < width)
+    deep = 3 * hidden_local
+    for row in range(2 * slab):
+        line = first_row + row + 1
+        keep = inside & (line >= 0) & (line < height)
+        stack = taps_ref[pl.ds(row * span, 3 * span), :]
+        for part in range(groups):
+            value = lax.dot_general(
+                win_ref[part], stack, (((0,), (0,)), ((), ())), preferred_element_type=jnp.float32
+            )
+            value = jnp.maximum(value + bias_ref[pl.ds(part * hidden_local, hidden_local), :], 0.0)
+            value = jnp.where(keep, value, 0.0)
+            for off in range(3):
+                moved = value if off == 0 else pltpu.roll(value, wide - off, 1)
+                hidden_ref[part, pl.ds(row * deep + off * hidden_local, hidden_local), :] = moved[
+                    :, :block
+                ].astype(jnp.bfloat16)
+    share = unmix_ref.shape[0] // groups
+    for row in range(slab):
+        raw = bout_ref[...] + jnp.zeros((2 * half, block), jnp.float32)
+        for part in range(groups):
+            raw = raw + jnp.dot(
+                wout_ref[part],
+                hidden_ref[part, pl.ds(row * deep, 3 * deep), :],
+                preferred_element_type=jnp.float32,
+            )
+        latent = zb_ref[row].astype(jnp.float32)
+        coupled = (latent - raw[half:]) * jnp.exp(-jnp.tanh(raw[:half]))
+        own = pltpu.roll(za_ref[slab + row].astype(jnp.float32), wide - 2, 1)[:, :block]
+        joined = jnp.concatenate([own, coupled], axis=0)
+        mixed = jnp.dot(
+            unmix_ref[...],
+            joined,
+            precision=lax.Precision.HIGHEST,
+            preferred_element_type=jnp.float32,
+        )
+        for part in range(groups):
+            out_ref[part, pl.ds(row * share, share), :] = mixed[part * share : (part + 1) * share]
+
+
+def couple(za_ext, latent, w_in, w_out, bias, b_out, unmix, dims):
+    slab, half, quarter, hidden_local, groups, block, width, height = dims
+    wide = za_ext.shape[2]
+    chans = unmix.shape[0]
+
+    def kernel(*refs):
+        couple_kernel(dims, *refs)
+
+    return pl.pallas_call(
+        kernel,
+        out_shape=jax.ShapeDtypeStruct((groups, slab * chans // groups, block), jnp.float32),
+        in_specs=[vmem] * 7,
+        out_specs=vmem,
+        scratch_shapes=[
+            pltpu.VMEM((3 * slab * 3 * half, wide), jnp.bfloat16),
+            pltpu.VMEM((groups, 2 * slab * 3 * hidden_local, block), jnp.bfloat16),
+        ],
+        name="couple_and_mix",
+    )(za_ext, latent, w_in, w_out, bias, b_out, unmix)
 
 
 def halves(values):
@@ -297,40 +362,24 @@
     za_got, zb_got, w_in_all, w_out_all, bias = gather(
         za_cols, zb_cols, w_in_parts, w_out_parts, b_in[None, :], rows, groups, 2
     )
-    za_ext = za_got.reshape(3, groups, slab, quarter, block + 128)[..., : block + 4]
-    za_ext = za_ext.transpose(0, 2, 1, 3, 4).reshape(3 * slab, half, block + 4)
+    za_ext = za_got.reshape(3, groups, slab, quarter, block + 128)
+    za_ext = za_ext.transpose(0, 2, 1, 3, 4).reshape(3 * slab, half, block + 128)
     ext_rows = row_idx * slab - slab + jnp.arange(3 * slab, dtype=jnp.int32)
     inside = (ext_rows >= 0) & (ext_rows < height)
     za_ext = jnp.where(inside[:, None, None], za_ext, jnp.zeros((), za.dtype))
-    ext_cols = chan_idx * block - 1 + jnp.arange(block + 2, dtype=jnp.int32)
-    inside_cols = (ext_cols >= 0) & (ext_cols < width)
-    hidden_units = groups * hidden_local
-    hidden = jnp.einsum(
-        "rkcw,qkco->rqow",
-        taps_of(za_ext, block + 2),
-        w_in_all.reshape(groups, taps, half, hidden_local),
-        preferred_element_type=jnp.float32,
-    ).reshape(2 * slab, hidden_units, block + 2)
-    hidden = jax.nn.relu(hidden + bias.reshape(hidden_units)[None, :, None])
-    keep = inside[1:-1][:, None, None] & inside_cols[None, None, :]
-    hidden = jnp.where(keep, hidden, 0.0).astype(jnp.bfloat16)
-    hidden_taps = taps_of(hidden, block).reshape(slab, taps, groups, hidden_local, block)
-    raw = jnp.einsum(
-        "rkqcw,qokc->row",
-        hidden_taps,
-        w_out_all.reshape(groups, chans, taps, hidden_local),
-        preferred_element_type=jnp.float32,
-    )
-    raw = raw + b_out.reshape(chans)[None, :, None]
     latent = zb_got.reshape(groups, slab, quarter, block).transpose(1, 0, 2, 3)
-    latent = latent.reshape(slab, half, block).astype(jnp.float32)
-    coupled = (latent - raw[:, half:]) * jnp.exp(-jnp.tanh(raw[:, :half]))
-    za_own = za_ext[slab : 2 * slab, :, 2 : 2 + block]
-    joined = jnp.concatenate([za_own.astype(jnp.float32), coupled], axis=1)
-    mixed = jnp.einsum("oc,rcw->row", unmix, joined, precision=lax.Precision.HIGHEST)
-    mixed = mixed.reshape(slab, groups, mine, block).transpose(1, 0, 2, 3)
+    mixed = couple(
+        za_ext,
+        latent.reshape(slab, half, block),
+        w_in_all.reshape(groups, taps * half, hidden_local),
+        w_out_all.reshape(groups, chans, taps * hidden_local),
+        bias.reshape(groups * hidden_local, 1),
+        b_out.reshape(chans, 1),
+        unmix,
+        (slab, half, quarter, hidden_local, groups, block, width, height),
+    )
     mixed = swap(mixed, "chan", 1)
-    mixed = mixed.transpose(1, 2, 0, 3).reshape(slab * mine, width)
+    mixed = mixed.transpose(1, 0, 2).reshape(slab * mine, width)
 
     packed = dot3(mixed, table, 0)
     outgoing = packed.reshape(slab, chan_groups, triple, freq_groups, lanes)

time: 151 us -> 126 us (0.83)
  local copies, waits for them, and re-layouts: 45.1 us -> 19.1 us
  Pallas kernels: 88.9 us -> 94.5 us
  matrix products: 11.1 us -> 6.78 us
    unnamed x61 -> x35, local copies, waits for them, and re-layouts: 15.8 us -> 4.15 us
    slice x11 -> x0, local copies, waits for them, and re-layouts: 9.85 us -> none  [the longest x10 9.77 us: taps_of(): source[row_off:row_off + rows_out, :, col_off:col_off + width]]
    pallas_call x0 -> x1, Pallas kernels: none -> 5.71 us  [couple(): pl.pallas_call(kernel, out_shape=jax.ShapeDtypeStruct((groups, slab * cha...]
    dot_general x3 -> x0, matrix products: 4.27 us -> none  [the longest x1 3.12 us: on_device(): jnp.einsum('rkqcw,qokc->row', hidden_taps, w_out_all.reshape(groups, chan...]
    transpose x4 -> x2, local copies, waits for them, and re-layouts: 3.9 us -> 0.08 us  [the longest x1 0.04 us: on_device(): latent = zb_got.reshape(groups, slab, quarter, block).transpose(1, 0, 2, 3)]
    reshape x4 -> x5, local copies, waits for them, and re-layouts: 3.4 us -> 3.9 us  [the longest x1 1.53 us: on_device(): bias.reshape(groups * hidden_local, 1)]
where the time goes in v3:
time: 126 us; the launch traced here: 125 us
  Pallas kernels  94.5 us (75%)
  local copies, waits for them, and re-layouts  19.1 us (15%)
  matrix products  6.78 us (5%)
  other arithmetic  4.45 us (4%)
    pallas_call x3, Pallas kernels, swap(): pl.pallas_call(kernel, out_shape=jax.ShapeDtypeStruct(x.shape, x.dtype),...  61.8 us
    pallas_call x1, Pallas kernels, gather(): pl.pallas_call(kernel, out_shape=(several((3,), za_cols), several((), zb_...  27.1 us
    pallas_call x1, Pallas kernels, couple(): pl.pallas_call(kernel, out_shape=jax.ShapeDtypeStruct((groups, slab * cha...  5.71 us
    dot_general x4, matrix products, dot(): lax.dot_general(a, b, (((1,), (contract,)), ((), ())), preferred_element_...  4.73 us
    unnamed x35, local copies, waits for them, and re-layouts  4.15 us

profile of v3, /device:TPU:1, one launch (start us, length us, event | category | flops | bytes accessed | tf_op | source)
XLA Modules:
  0.0 125.4 jit_solution(18380242672910418643)
XLA Ops:
  0.0 0.8 copy.50
  1.0 0.6 pad_maximum_fusion.1.refs_0_
  1.6 1.1 copy.53
  2.7 0.9 reshape.214
  3.6 0.8 copy.51
  4.4 0.6 copy.95
  5.1 27.1 %gather_inputs.1 = (bf16[3,4,24,384]{3,2,1,0:T(8,128)(2,1)}, bf16[4,24,256]{2,1,0:T(8,128)(2,1)}, bf16[4,2,216,128]{3,2,1,0:T(8,128)(2,1)}, bf16[4,2,48,1152]{3,2,1,0:T(8,128)(2,1)}, f32[4,1,128]{2,1,0:T(1,128)}) custom-call(bf16[4,24,384]{2,1,0:T(8,128)(2,1)} %pad_maximum_fusion.1.refs_0_, bf16[4,24,256]{2,1,0:T(8,128)(2,1)} %bitcast.140, ...), custom_call_target="tpu_custom_call" | custom-call | tf_op jit(solution)/shard_map/gather_inputs/pallas_call | solution.py:197
  32.1 1.0 copy.54
  33.4 0.8 broadcast_select_fusion.refs_0_
  34.1 1.5 %copy.59.refs_4_ = f32[512,1]{1,0:T(8,128)} copy(f32[512,1]{0,1:T(1,128)} %bitcast.143) | data formatting | bytes 4096 | tf_op jit(solution)/shard_map/reshape | solution.py:376
  35.8 0.6 copy.58.refs_1_
  36.4 0.7 reshape.240.refs_5_
  37.1 5.7 %couple_and_mix.1.refs_0_ = f32[4,48,256]{2,1,0:T(8,128)} custom-call(bf16[6,48,384]{2,1,0:T(8,128)(2,1)} %broadcast_select_fusion.refs_0_, bf16[2,48,256]{2,1,0:T(8,128)(2,1)} %copy.58.refs_1_, bf16[4,432,128]{2,1,0:T(8,128)(2,1)} %bitcast.136, bf16[4,96,1152]{2,1,0:T(8,128)(2,1)} %bitcast.131, f32[512,1]{1,0:T(8,128)} %copy.59.refs_4_, ...), custom_call_target="tpu_custom_call" | custom-call | tf_op jit(solution)/shard_map/couple_and_mix/pallas_call | solution.py:282
  42.8 10.7 %swap_chan1.1 = f32[4,48,256]{2,1,0:T(8,128)} custom-call(f32[4,48,256]{2,1,0:T(8,128)} %couple_and_mix.1.refs_0_), custom_call_target="tpu_custom_call" | custom-call | tf_op jit(solution)/shard_map/swap_chan1/pallas_call | solution.py:67
  53.6 0.9 copy.80
  54.6 1.2 reduce-precision_convert_fusion
  55.8 1.3 %copy-done.1 = bf16[32,32,1024]{2,1,0:T(8,128)(2,1)} copy-done((bf16[32,32,1024]{2,1,0:T(8,128)(2,1)}, bf16[32,32,1024]{2,1,0:T(8,128)(2,1)S(1)}, u32[]{:S(2)}) %copy-start.1) | copy-done | bytes 2097176
  57.1 0.5 fusion.4
  57.6 0.5 convolution_add_fusion.2
  58.8 0.8 copy.64.refs_0_
  59.6 28.3 %swap_rows3.1 = f32[128,3,128]{2,1,0:T(4,128)} custom-call(f32[128,3,128]{2,1,0:T(4,128)} %copy.64.refs_0_), custom_call_target="tpu_custom_call" | custom-call | tf_op jit(solution)/shard_map/swap_rows3/pallas_call | solution.py:67
  87.9 1.1 copy.65
  89.0 0.7 fusion.20
  89.9 1.4 %fusion.29 = f32[512,384]{0,1:T(8,128)} fusion(f32[512,256]{1,0:T(8,128)S(1)} %copy-done.3, f32[256,384]{0,1:T(8,128)S(1)} %bitcast.129), kind=kOutput, calls=%fused_computation.81 | convolution fusion | flops 301989888 | bytes 1703936 | tf_op jit(solution)/shard_map/dot_general | solution.py:405
  91.3 1.7 %reshape.231 = f32[2,256,3,2,64]{1,0,4,3,2:T(2,128)S(1)} reshape(f32[512,384]{0,1:T(8,128)} %fusion.29) | data formatting | bytes 1572864 | tf_op jit(solution)/shard_map/reshape | solution.py:407
  93.0 0.4 slice_add_fusion.1
  93.9 0.7 fusion.22
  96.1 0.8 copy.69.refs_0_
  96.9 22.8 %swap_rows4.1 = f32[128,3,128]{2,1,0:T(4,128)} custom-call(f32[128,3,128]{2,1,0:T(4,128)} %copy.69.refs_0_), custom_call_target="tpu_custom_call" | custom-call | tf_op jit(solution)/shard_map/swap_rows4/pallas_call | solution.py:67
  119.7 1.2 reshape.241
  121.3 2.4 %fusion.8 = f32[96,1024]{1,0:T(8,128)S(1)} fusion(bf16[1024,1024]{1,0:T(8,128)(2,1)} %bitcast.123, bf16[48,1024]{1,0:T(8,128)(2,1)S(1)} %get-tuple-element.30, bf16[48,1024]{1,0:T(8,128)(2,1)S(1)} %get-tuple-element.29), kind=kOutput, calls=%fused_computation.29 | convolution fusion | flops 201719808 | bytes 2686976 | tf_op jit(solution)/shard_map/dot_general | solution.py:325
  124.0 1.4 %convolution_add_fusion = f32[48,1024]{1,0:T(8,128)} fusion(bf16[48,1024]{1,0:T(8,128)(2,1)S(1)} %convert_element_type.57, bf16[1024,1024]{1,0:T(8,128)(2,1)S(1)} %bitcast.121, f32[96,1024]{1,0:T(8,128)S(1)} %fusion.8), kind=kOutput, calls=%fused_computation.4 | convolution fusion | flops 100761600 | bytes 2785280 | tf_op jit(solution)/shard_map/dot_general | solution.py:325
  (73 shorter events, 3.7 us)
Async XLA Ops:
  0.0 93.4 %copy-start = (f32[3,3,96]{2,1,0:T(4,128)S(1)}, f32[3,3,96]{2,1,0:T(4,128)}, u32[]{:S(2)}) copy-start(f32[3,3,96]{2,1,0:T(4,128)} %param.27) | copy-start | bytes 10372
  1.6 34.8 %copy-start.13 = (f32[2,48]{1,0:T(2,128)S(1)}, f32[2,48]{1,0:T(2,128)}, u32[]{:S(2)}) copy-start(f32[2,48]{1,0:T(2,128)} %param.25) | copy-start | bytes 1156
  32.1 3.6 %copy-start.10 = (bf16[4,24,256]{2,1,0:T(8,128)(2,1)S(1)}, bf16[4,24,256]{2,1,0:T(8,128)(2,1)}, u32[]{:S(2)}) copy-start(bf16[4,24,256]{2,1,0:T(8,128)(2,1)} %get-tuple-element.15) | copy-start | bytes 147460
  33.3 21.2 %copy-start.6 = (f32[32,1024]{1,0:T(8,128)S(1)}, f32[32,1024]{1,0:T(8,128)}, u32[]{:S(2)}) copy-start(f32[32,1024]{1,0:T(8,128)} %constant.88.clone) | copy-start | bytes 393220
  33.3 21.2 %copy-start.7 = (f32[32,1024]{1,0:T(8,128)S(1)}, f32[32,1024]{1,0:T(8,128)}, u32[]{:S(2)}) copy-start(f32[32,1024]{1,0:T(8,128)} %constant.89.clone) | copy-start | bytes 393220
  33.3 21.2 %copy-start.8 = (f32[32,1024]{1,0:T(8,128)S(1)}, f32[32,1024]{1,0:T(8,128)}, u32[]{:S(2)}) copy-start(f32[32,1024]{1,0:T(8,128)} %constant.90.clone) | copy-start | bytes 393220
  33.3 21.2 %copy-start.9 = (f32[32,1024]{1,0:T(8,128)S(1)}, f32[32,1024]{1,0:T(8,128)}, u32[]{:S(2)}) copy-start(f32[32,1024]{1,0:T(8,128)} %constant.91.clone) | copy-start | bytes 393220
  55.7 1.3 %copy-start.1 = (bf16[32,32,1024]{2,1,0:T(8,128)(2,1)}, bf16[32,32,1024]{2,1,0:T(8,128)(2,1)S(1)}, u32[]{:S(2)}) copy-start(bf16[32,32,1024]{2,1,0:T(8,128)(2,1)S(1)} %get-tuple-element.25) | copy-start | bytes 6291460
  55.7 1.8 %copy-start.2 = (f32[4,48,256]{2,1,0:T(8,128)S(1)}, f32[4,48,256]{2,1,0:T(8,128)}, u32[]{:S(2)}) copy-start(f32[4,48,256]{2,1,0:T(8,128)} %swap_chan1.1) | copy-start | bytes 589828
  58.5 31.4 %copy-start.3 = (f32[512,256]{1,0:T(8,128)S(1)}, f32[512,256]{1,0:T(8,128)}, u32[]{:S(2)}) copy-start(f32[512,256]{1,0:T(8,128)} %constant.93.clone) | copy-start | bytes 1572868
  91.3 3.7 %copy-start.11 = (f32[256]{0:T(256)S(1)}, f32[256]{0:T(256)}, u32[]{:S(2)}) copy-start(f32[256]{0:T(256)} %constant.96.clone) | copy-start | bytes 3076
  91.3 3.7 %copy-start.12 = (f32[256]{0:T(256)S(1)}, f32[256]{0:T(256)}, u32[]{:S(2)}) copy-start(f32[256]{0:T(256)} %constant.97.clone) | copy-start | bytes 3076
  91.3 4.0 %copy-start.5 = (f32[256,256]{1,0:T(8,128)S(1)}, f32[256,256]{1,0:T(8,128)}, u32[]{:S(2)}) copy-start(f32[256,256]{1,0:T(8,128)} %constant.108) | copy-start | bytes 786436
  92.9 2.7 %copy-start.4 = (f32[256,256]{1,0:T(8,128)S(1)}, f32[256,256]{1,0:T(8,128)}, u32[]{:S(2)}) copy-start(f32[256,256]{1,0:T(8,128)} %constant.109) | copy-start | bytes 786436

commit v4 on v3

--- a/solution.py
+++ b/solution.py
@@ -11,72 +11,6 @@
 full_turn = 2.0 * math.pi
 vmem = pl.BlockSpec(memory_space=pltpu.VMEM)
 mesh_ids = pl.DeviceIdType.MESH
-
-
-def swap_kernel(axis, count, x_ref, out_ref, send_sem, recv_sem, own_sem):
-    me_row = lax.axis_index("rows")
-    me_chan = lax.axis_index("chan")
-    me = me_row if axis == "rows" else me_chan
-
-    def place(peer):
-        return (peer, me_chan) if axis == "rows" else (me_row, peer)
-
-    barrier = pltpu.get_barrier_semaphore()
-
-    def greet(step, carry):
-        pl.semaphore_signal(
-            barrier, inc=1, device_id=place(lax.rem(me + step, count)), device_id_type=mesh_ids
-        )
-        return carry
-
-    lax.fori_loop(1, count, greet, 0)
-    own = pltpu.make_async_copy(x_ref.at[me], out_ref.at[me], own_sem)
-    own.start()
-    pl.semaphore_wait(barrier, count - 1)
-
-    def copy(step):
-        peer = lax.rem(me + step, count)
-        return pltpu.make_async_remote_copy(
-            src_ref=x_ref.at[peer],
-            dst_ref=out_ref.at[me],
-            send_sem=send_sem.at[step],
-            recv_sem=recv_sem.at[step],
-            device_id=place(peer),
-            device_id_type=mesh_ids,
-        )
-
-    def start(step, carry):
-        copy(step).start()
-        return carry
-
-    def finish(step, carry):
-        copy(step).wait()
-        return carry
-
-    lax.fori_loop(1, count, start, 0)
-    own.wait()
-    lax.fori_loop(1, count, finish, 0)
-
-
-def swap(x, axis, ident):
-    count = x.shape[0]
-
-    def kernel(*refs):
-        swap_kernel(axis, count, *refs)
-
-    return pl.pallas_call(
-        kernel,
-        out_shape=jax.ShapeDtypeStruct(x.shape, x.dtype),
-        in_specs=[vmem],
-        out_specs=vmem,
-        scratch_shapes=[
-            pltpu.SemaphoreType.DMA((count,)),
-            pltpu.SemaphoreType.DMA((count,)),
-            pltpu.SemaphoreType.DMA,
-        ],
-        compiler_params=pltpu.CompilerParams(collective_id=ident, has_side_effects=True),
-        name="swap_" + axis + str(ident),
-    )(x)
 
 
 def gather_kernel(rows, chans, halves_of, *refs):
@@ -217,10 +151,16 @@
     )(za_cols, zb_cols, w_in, w_out, bias)
 
 
-def couple_kernel(dims, *refs):
+def as_column(line):
+    size = line.shape[1]
+    down = lax.broadcasted_iota(jnp.int32, (size, size), 0)
+    along = lax.broadcasted_iota(jnp.int32, (size, size), 1)
+    return jnp.sum(jnp.where(down == along, line, 0.0), axis=1, keepdims=True)
+
+
+def couple_kernel(dims, refs, taps_ref, hidden_ref):
     slab, half, quarter, hidden_local, groups, block, width, height = dims
-    za_ref, zb_ref, win_ref, wout_ref, bias_ref, bout_ref, unmix_ref, out_ref = refs[:8]
-    taps_ref, hidden_ref = refs[8:]
+    za_ref, zb_ref, win_ref, wout_ref, bias_ref, bout_ref, unmix_ref, out_ref = refs
     wide = za_ref.shape[2]
     first_row = lax.axis_index("rows") * slab - slab
     first_col = lax.axis_index("chan") * block - 1
@@ -233,15 +173,17 @@
     cols = first_col + lax.broadcasted_iota(jnp.int32, (hidden_local, wide), 1)
     inside = (cols >= 0) & (cols < width)
     deep = 3 * hidden_local
+    biases = [as_column(bias_ref[part]) for part in range(groups)]
+    out_bias = as_column(bout_ref[...])
     for row in range(2 * slab):
         line = first_row + row + 1
         keep = inside & (line >= 0) & (line < height)
         stack = taps_ref[pl.ds(row * span, 3 * span), :]
         for part in range(groups):
             value = lax.dot_general(
-                win_ref[part], stack, (((0,), (0,)), ((), ())), preferred_element_type=jnp.float32
-            )
-            value = jnp.maximum(value + bias_ref[pl.ds(part * hidden_local, hidden_local), :], 0.0)
+                win_ref[part], stack, (((1,), (0,)), ((), ())), preferred_element_type=jnp.float32
+            )
+            value = jnp.maximum(value + biases[part], 0.0)
             value = jnp.where(keep, value, 0.0)
             for off in range(3):
                 moved = value if off == 0 else pltpu.roll(value, wide - off, 1)
@@ -250,7 +192,7 @@
                 ].astype(jnp.bfloat16)
     share = unmix_ref.shape[0] // groups
     for row in range(slab):
-        raw = bout_ref[...] + jnp.zeros((2 * half, block), jnp.float32)
+        raw = out_bias + jnp.zeros((2 * half, block), jnp.float32)
         for part in range(groups):
             raw = raw + jnp.dot(
                 wout_ref[part],
@@ -271,25 +213,227 @@
             out_ref[part, pl.ds(row * share, share), :] = mixed[part * share : (part + 1) * share]
 
 
-def couple(za_ext, latent, w_in, w_out, bias, b_out, unmix, dims):
+def split(values):
+    high = values.astype(jnp.bfloat16)
+    return high, (values - high.astype(jnp.float32)).astype(jnp.bfloat16)
+
+
+def main_kernel(dims, counts, *refs):
     slab, half, quarter, hidden_local, groups, block, width, height = dims
-    wide = za_ext.shape[2]
-    chans = unmix.shape[0]
+    rows, triple, lanes = counts
+    couple_refs = refs[:7]
+    thigh_ref, tlow_ref, fhigh_ref, flow_ref, bhigh_ref, blow_ref = refs[7:13]
+    near_ref, turn_ref, lane_ref, out_ref = refs[13:17]
+    taps_ref, hidden_ref, mix_ref, mixed_ref, send_ref, got_ref, back_ref, home_ref = refs[17:25]
+    work_ref, own_sem, chan_sem, there_sem, back_sem = refs[25:]
+    mine = 2 * half // groups
+    tile = 2 * lanes
+    freq_groups = width // lanes
+    chan_groups = rows // freq_groups
+    me_row = lax.axis_index("rows")
+    me_chan = lax.axis_index("chan")
+    barrier = pltpu.get_barrier_semaphore()
+
+    def greet(step, carry):
+        pl.semaphore_signal(
+            barrier,
+            inc=1,
+            device_id=(lax.rem(me_row + step, rows), me_chan),
+            device_id_type=mesh_ids,
+        )
+        return carry
+
+    for step in range(1, groups):
+        pl.semaphore_signal(
+            barrier,
+            inc=1,
+            device_id=(me_row, lax.rem(me_chan + step, groups)),
+            device_id_type=mesh_ids,
+        )
+    lax.fori_loop(1, rows, greet, 0)
+    couple_kernel(dims, tuple(couple_refs) + (mix_ref,), taps_ref, hidden_ref)
+    pl.semaphore_wait(barrier, rows - 1 + groups - 1)
+
+    swaps = []
+    for step in range(1, groups):
+        peer = lax.rem(me_chan + step, groups)
+        swaps.append(
+            pltpu.make_async_remote_copy(
+                src_ref=mix_ref.at[peer],
+                dst_ref=mixed_ref.at[me_chan],
+                send_sem=chan_sem.at[0, step],
+                recv_sem=chan_sem.at[1, step],
+                device_id=(me_row, peer),
+                device_id_type=mesh_ids,
+            )
+        )
+    for one in swaps:
+        one.start()
+    own = pltpu.make_async_copy(mix_ref.at[me_chan], mixed_ref.at[me_chan], own_sem.at[0])
+    own.start()
+    own.wait()
+    for one in swaps:
+        one.wait()
+
+    high, low = split(jnp.concatenate([mixed_ref[i] for i in range(groups)], axis=1))
+    lead = slab * mine
+    both = jnp.dot(
+        jnp.concatenate([high, low], axis=0), thigh_ref[...], preferred_element_type=jnp.float32
+    )
+    packed = both[:lead] + both[lead:]
+    packed = packed + jnp.dot(high, tlow_ref[...], preferred_element_type=jnp.float32)
+    lane = lax.broadcasted_iota(jnp.int32, (mine, tile), 1)
+    for pair in range(freq_groups // 2):
+        first = packed[:mine, pair * tile : (pair + 1) * tile]
+        second = packed[mine:, pair * tile : (pair + 1) * tile]
+        even = jnp.where(lane < lanes, first, pltpu.roll(second, lanes, 1))
+        odd = jnp.where(lane < lanes, pltpu.roll(first, lanes, 1), second)
+        for which, value in ((2 * pair, even), (2 * pair + 1, odd)):
+            for group in range(chan_groups):
+                send_ref[which * chan_groups + group] = value[
+                    group * triple : (group + 1) * triple
+                ]
+
+    def exchange(source, target, sems, own_at):
+        def copy(step):
+            peer = lax.rem(me_row + step, rows)
+            return pltpu.make_async_remote_copy(
+                src_ref=source.at[peer],
+                dst_ref=target.at[me_row],
+                send_sem=sems.at[0, step],
+                recv_sem=sems.at[1, step],
+                device_id=(peer, me_chan),
+                device_id_type=mesh_ids,
+            )
+
+        def start(step, carry):
+            copy(step).start()
+            return carry
+
+        def finish(step, carry):
+            copy(step).wait()
+            return carry
+
+        lax.fori_loop(1, rows, start, 0)
+        kept = pltpu.make_async_copy(source.at[me_row], target.at[me_row], own_sem.at[own_at])
+        kept.start()
+        kept.wait()
+        lax.fori_loop(1, rows, finish, 0)
+
+    exchange(send_ref, got_ref, there_sem, 1)
+
+    lane = lax.broadcasted_iota(jnp.int32, (rows, tile), 1)
+    sign = lane_ref[pl.ds(0, 1), :]
+    scale = lane_ref[pl.ds(1, 1), :]
+    stacks = []
+    for chan in range(triple):
+        data = got_ref[:, chan, :]
+        other = jnp.where(
+            lax.rem(lane, lanes) < lanes // 2,
+            pltpu.roll(data, tile - lanes // 2, 1),
+            pltpu.roll(data, lanes // 2, 1),
+        )
+        stacks.append(jnp.concatenate([data, other * sign], axis=0))
+    high, low = split(jnp.concatenate(stacks, axis=1))
+    forward = jnp.dot(fhigh_ref[...], high, preferred_element_type=jnp.float32)
+    forward = forward + jnp.dot(fhigh_ref[...], low, preferred_element_type=jnp.float32)
+    forward = forward + jnp.dot(flow_ref[...], high, preferred_element_type=jnp.float32)
+    cos_u = turn_ref[0]
+    sin_u = turn_ref[1]
+    solved = []
+    for chan in range(triple):
+        piece = forward[:, chan * tile : (chan + 1) * tile]
+        parts = [piece[i * height : (i + 1) * height] for i in range(4)]
+        real_part = parts[0] + pltpu.roll(parts[1], lanes, 1)
+        imag_part = parts[2] + pltpu.roll(parts[3], lanes, 1)
+        near = [near_ref[i, pl.ds(chan, 1), :] for i in range(6)]
+        symbol_real = near[1] + (near[0] + near[2]) * cos_u + (near[3] - near[5]) * sin_u
+        symbol_imag = near[4] + (near[3] + near[5]) * cos_u + (near[2] - near[0]) * sin_u
+        factor = scale / (symbol_real * symbol_real + symbol_imag * symbol_imag)
+        solved.append(
+            jnp.concatenate(
+                [
+                    (real_part * symbol_real + imag_part * symbol_imag) * factor,
+                    (imag_part * symbol_real - real_part * symbol_imag) * factor,
+                ],
+                axis=0,
+            )
+        )
+    high, low = split(jnp.concatenate(solved, axis=1))
+    inverse = jnp.dot(bhigh_ref[...], high, preferred_element_type=jnp.float32)
+    inverse = inverse + jnp.dot(bhigh_ref[...], low, preferred_element_type=jnp.float32)
+    inverse = inverse + jnp.dot(blow_ref[...], high, preferred_element_type=jnp.float32)
+    for chan in range(triple):
+        piece = inverse[:, chan * tile : (chan + 1) * tile]
+        back_ref[:, chan, :] = jnp.where(
+            lane < lanes, piece[:rows], pltpu.roll(piece[rows:], lanes, 1)
+        )
+
+    exchange(back_ref, home_ref, back_sem, 2)
+
+    for which in range(rows):
+        work_ref[which // chan_groups, pl.ds(which % chan_groups * triple, triple), :] = home_ref[
+            which
+        ]
+    lane = lax.broadcasted_iota(jnp.int32, (mine, tile), 1)
+    upper = []
+    lower = []
+    for pair in range(freq_groups // 2):
+        even = work_ref[2 * pair]
+        odd = work_ref[2 * pair + 1]
+        upper.append(jnp.where(lane < lanes, even, pltpu.roll(odd, lanes, 1)))
+        lower.append(jnp.where(lane < lanes, pltpu.roll(even, lanes, 1), odd))
+    final = jnp.concatenate(
+        [jnp.concatenate(upper, axis=1), jnp.concatenate(lower, axis=1)], axis=0
+    )
+    high, low = split(final)
+
+    def across(values, table):
+        return lax.dot_general(
+            values, table[...], (((1,), (1,)), ((), ())), preferred_element_type=jnp.float32
+        )
+
+    both = across(jnp.concatenate([high, low], axis=0), thigh_ref)
+    result = both[:lead] + both[lead:] + across(high, tlow_ref)
+    for row in range(slab):
+        out_ref[row] = result[row * mine : (row + 1) * mine]
+
+
+def whole(operands, dims, counts):
+    slab, half, quarter, hidden_local, groups, block, width, height = dims
+    rows, triple, lanes = counts
+    wide = operands[0].shape[2]
+    mine = 2 * half // groups
+    tile = 2 * lanes
 
     def kernel(*refs):
-        couple_kernel(dims, *refs)
-
+        main_kernel(dims, counts, *refs)
+
+    mix = pltpu.VMEM((groups, slab * mine, block), jnp.float32)
+    message = pltpu.VMEM((rows, triple, tile), jnp.float32)
     return pl.pallas_call(
         kernel,
-        out_shape=jax.ShapeDtypeStruct((groups, slab * chans // groups, block), jnp.float32),
-        in_specs=[vmem] * 7,
+        out_shape=jax.ShapeDtypeStruct((slab, mine, width), jnp.float32),
+        in_specs=[vmem] * len(operands),
         out_specs=vmem,
         scratch_shapes=[
             pltpu.VMEM((3 * slab * 3 * half, wide), jnp.bfloat16),
             pltpu.VMEM((groups, 2 * slab * 3 * hidden_local, block), jnp.bfloat16),
+            mix,
+            mix,
+            message,
+            message,
+            message,
+            message,
+            pltpu.VMEM((width // lanes, mine, tile), jnp.float32),
+            pltpu.SemaphoreType.DMA((3,)),
+            pltpu.SemaphoreType.DMA((2, groups)),
+            pltpu.SemaphoreType.DMA((2, rows)),
+            pltpu.SemaphoreType.DMA((2, rows)),
         ],
-        name="couple_and_mix",
-    )(za_ext, latent, w_in, w_out, bias, b_out, unmix)
+        compiler_params=pltpu.CompilerParams(collective_id=1, has_side_effects=True),
+        name="couple_and_solve",
+    )(*operands)
 
 
 def halves(values):
@@ -316,20 +460,6 @@
     return halves(table), freq, sign, weight
 
 
-def dot3(left, right_halves, contract):
-    high, low = halves(left)
-    right_high, right_low = right_halves
-    count = left.shape[0]
-
-    def dot(a, b):
-        return lax.dot_general(
-            a, b, (((1,), (contract,)), ((), ())), preferred_element_type=jnp.float32
-        )
-
-    both = dot(jnp.concatenate([high, low], axis=0), right_high)
-    return both[:count] + both[count:] + dot(high, right_low)
-
-
 def on_device(za, zb, w_in, b_in, w_out, b_out, unmix, kern):
     slab, quarter, width = za.shape
     hidden_local = w_in.shape[3]
@@ -355,7 +485,9 @@
         [za_wide[:, block * i : block * i + block + 128] for i in range(groups)], axis=0
     )
     taps = 9
-    w_in_parts = w_in.reshape(2, taps * half // 2, hidden_local)
+    w_in_parts = w_in.reshape(taps * half, hidden_local).T.reshape(
+        2, hidden_local // 2, taps * half
+    )
     w_out_parts = w_out.reshape(taps * hidden_local, chans).T.reshape(
         2, chans // 2, taps * hidden_local
     )
@@ -368,73 +500,55 @@
     inside = (ext_rows >= 0) & (ext_rows < height)
     za_ext = jnp.where(inside[:, None, None], za_ext, jnp.zeros((), za.dtype))
     latent = zb_got.reshape(groups, slab, quarter, block).transpose(1, 0, 2, 3)
-    mixed = couple(
-        za_ext,
-        latent.reshape(slab, half, block),
-        w_in_all.reshape(groups, taps * half, hidden_local),
-        w_out_all.reshape(groups, chans, taps * hidden_local),
-        bias.reshape(groups * hidden_local, 1),
-        b_out.reshape(chans, 1),
-        unmix,
-        (slab, half, quarter, hidden_local, groups, block, width, height),
-    )
-    mixed = swap(mixed, "chan", 1)
-    mixed = mixed.transpose(1, 0, 2).reshape(slab * mine, width)
-
-    packed = dot3(mixed, table, 0)
-    outgoing = packed.reshape(slab, chan_groups, triple, freq_groups, lanes)
-    outgoing = outgoing.transpose(3, 1, 2, 0, 4).reshape(rows, triple, slab * lanes)
-    got = swap(outgoing, "rows", 3)
-    data = got.reshape(rows, triple, slab, lanes).transpose(2, 0, 1, 3)
-    data = data.reshape(height, triple, lanes)
-
     freq_idx = row_idx // chan_groups
     chan_first = chan_idx * mine + row_idx % chan_groups * triple
-
-    def own_lanes(values):
-        grouped = jnp.asarray(values).reshape(freq_groups, lanes)
-        return lax.dynamic_index_in_dim(grouped, freq_idx, 0, keepdims=False)
-
-    sign_own = own_lanes(sign)
-    other = jnp.concatenate([data[..., lanes // 2 :], data[..., : lanes // 2]], axis=2)
-    pair = jnp.concatenate([data, other * sign_own], axis=2).reshape(height, triple * 2 * lanes)
-    order = (np.arange(rows)[None, :] * slab + np.arange(slab)[:, None]).reshape(-1)
-    angles = np.arange(height)[:, None] * order[None, :] % height * (full_turn / height)
-    cosine = np.cos(angles).astype(np.float32)
-    sine = np.sin(angles).astype(np.float32)
-    both = jnp.dot(
-        jnp.asarray(np.concatenate([cosine, sine], axis=0)), pair, precision=lax.Precision.HIGH
-    ).reshape(2, height, triple, 2, lanes)
-    real_part = both[0, :, :, 0] + both[1, :, :, 1]
-    imag_part = both[0, :, :, 1] - both[1, :, :, 0]
-
     turn = freq * (full_turn / width)
-    cos_v = own_lanes(np.cos(turn).astype(np.float32))[None, None, :]
-    sin_v = own_lanes(np.sin(turn).astype(np.float32))[None, None, :]
+    lane_rows = np.stack([sign, weight * (1.0 / (height * width)), np.cos(turn), np.sin(turn)])
+    lane_rows = lane_rows.astype(np.float32).reshape(4, freq_groups, lanes).transpose(1, 0, 2)
+    lane_rows = np.concatenate([lane_rows, lane_rows], axis=2)
+    lane_own = lax.dynamic_index_in_dim(jnp.asarray(lane_rows), freq_idx, 0, keepdims=False)
+    cos_v = lane_own[2][None, None, :]
+    sin_v = lane_own[3][None, None, :]
     stencil = lax.dynamic_slice_in_dim(kern, chan_first, triple, 2)[..., None]
     near_real = stencil[:, 1] + (stencil[:, 0] + stencil[:, 2]) * cos_v
     near_imag = (stencil[:, 2] - stencil[:, 0]) * sin_v
+    near = jnp.concatenate([near_real, near_imag], axis=0)
     row_turn = np.arange(height) * (full_turn / height)
-    cos_u = jnp.asarray(np.cos(row_turn).astype(np.float32))[:, None, None]
-    sin_u = jnp.asarray(np.sin(row_turn).astype(np.float32))[:, None, None]
-    symbol_real = (
-        near_real[1] + (near_real[0] + near_real[2]) * cos_u + (near_imag[0] - near_imag[2]) * sin_u
-    )
-    symbol_imag = (
-        near_imag[1] + (near_imag[0] + near_imag[2]) * cos_u + (near_real[2] - near_real[0]) * sin_u
-    )
-    scale = own_lanes(weight) * (1.0 / (height * width))
-    factor = scale / (symbol_real * symbol_real + symbol_imag * symbol_imag)
-    solved_real = (real_part * symbol_real + imag_part * symbol_imag) * factor
-    solved_imag = (imag_part * symbol_real - real_part * symbol_imag) * factor
-    solved = jnp.concatenate([solved_real, solved_imag], axis=0).reshape(2 * height, triple * lanes)
-    back_table = np.concatenate([cosine.T, -sine.T], axis=1)
-    rows_back = jnp.dot(jnp.asarray(back_table), solved, precision=lax.Precision.HIGH)
-    rows_back = rows_back.reshape(slab, rows, triple, lanes).transpose(1, 2, 0, 3)
-    rows_back = swap(rows_back.reshape(rows, triple, slab * lanes), "rows", 4)
-    final = rows_back.reshape(freq_groups, chan_groups, triple, slab, lanes)
-    final = final.transpose(3, 1, 2, 0, 4).reshape(slab * mine, width)
-    return dot3(final, table, 1).reshape(slab, mine, width)
+    turns = np.stack([np.cos(row_turn), np.sin(row_turn)]).astype(np.float32)
+    turns = np.broadcast_to(turns[:, :, None], (2, height, 2 * lanes))
+
+    blocks = []
+    for row in range(slab):
+        order = np.arange(rows) * slab + row
+        angles = np.arange(height)[:, None] * order[None, :] % height * (full_turn / height)
+        blocks.append((np.cos(angles), np.sin(angles)))
+    ahead = [np.concatenate([c, t], axis=1) for c, t in blocks]
+    ahead += [np.concatenate([-t, c], axis=1) for c, t in blocks]
+    behind = [np.concatenate([c.T, -t.T], axis=1) for c, t in blocks]
+
+    def fixed(pieces):
+        values = np.concatenate(pieces, axis=0)
+        high = values.astype(jnp.bfloat16)
+        low = (values - high.astype(np.float64)).astype(jnp.bfloat16)
+        return jnp.asarray(high), jnp.asarray(low)
+
+    operands = (
+        za_ext,
+        latent.reshape(slab, half, block),
+        w_in_all.reshape(groups, hidden_local, taps * half),
+        w_out_all.reshape(groups, chans, taps * hidden_local),
+        bias,
+        b_out.reshape(1, chans),
+        unmix,
+        *table,
+        *fixed(ahead),
+        *fixed(behind),
+        near,
+        jnp.asarray(turns),
+        lane_own,
+    )
+    dims = (slab, half, quarter, hidden_local, groups, block, width, height)
+    return whole(operands, dims, (rows, triple, lanes))
 
 
 def solution(mesh):

time: 126 us -> 99.7 us (0.79)
  Pallas kernels: 94.5 us -> 79.1 us
  matrix products: 6.78 us -> 0 us
  local copies, waits for them, and re-layouts: 19.1 us -> 13.2 us
    pallas_call x4 -> x1, Pallas kernels: 67.5 us -> 51.6 us  [whole(): pl.pallas_call(kernel, out_shape=jax.ShapeDtypeStruct((slab, mine, width)...]
    dot_general x7 -> x0, matrix products: 6.78 us -> none  [the longest x4 4.73 us: dot(): lax.dot_general(a, b, (((1,), (contract,)), ((), ())), preferred_element_...]
    reshape x15 -> x2, local copies, waits for them, and re-layouts: 8.86 us -> 2.31 us  [the longest x1 1.66 us: on_device(): w_in.reshape(taps * half, hidden_local)]
    convert_element_type x4 -> x1, other arithmetic: 1.34 us -> 2.87 us  [halves(): return (high.astype(jnp.bfloat16), (values - high).astype(jnp.bfloat16))]
    squeeze x0 -> x1, local copies, waits for them, and re-layouts: none -> 1.26 us  [on_device(): lax.dynamic_index_in_dim(jnp.asarray(lane_rows), freq_idx, 0, keepdims=Fa...]
    unnamed x35 -> x21, local copies, waits for them, and re-layouts: 4.15 us -> 4.46 us
where the time goes in v4:
time: 99.7 us; the launch traced here: 98.1 us
  Pallas kernels  79.1 us (79%)
  local copies, waits for them, and re-layouts  13.2 us (13%)
  other arithmetic  5.62 us (6%)
    pallas_call x1, Pallas kernels, whole(): pl.pallas_call(kernel, out_shape=jax.ShapeDtypeStruct((slab, mine, width)...  51.6 us
    pallas_call x1, Pallas kernels, gather(): pl.pallas_call(kernel, out_shape=(several((3,), za_cols), several((), zb_...  27.5 us
    unnamed x21, local copies, waits for them, and re-layouts  4.46 us
    convert_element_type x1, other arithmetic, halves(): return (high.astype(jnp.bfloat16), (values - high).astype(jnp.bfloat16))  2.87 us

profile of v4, /device:TPU:1, one launch (start us, length us, event | category | flops | bytes accessed | tf_op | source)
XLA Modules:
  0.0 98.1 jit_solution(4542052054299983483)
XLA Ops:
  0.0 0.0 copy-start
  0.0 0.0 copy-start.3
  0.0 0.0 copy-start.4
  0.0 0.0 copy-start.6
  0.0 0.9 copy.23
  1.0 0.1 fusion.1
  1.1 0.6 pad_maximum_fusion.refs_0_
  1.7 0.8 copy.24
  2.6 0.6 copy.40
  3.2 1.7 %copy.26 = bf16[432,128]{0,1:T(8,128)(2,1)} copy(bf16[432,128]{1,0:T(8,128)(2,1)} %bitcast.58) | data formatting | bytes 221184 | tf_op jit(solution)/shard_map/reshape | solution.py:488
  4.8 1.1 %copy.27 = bf16[3,3,128,2,48]{2,1,0,4,3:T(4,128)(2,1)S(1)} copy(bf16[3,3,128,2,48]{2,4,3,1,0:T(8,128)(2,1)} %param.22) | data formatting | bytes 442368 | tf_op args[4]
  5.9 0.9 reshape.93
  6.8 27.5 %gather_inputs.1 = (bf16[3,4,24,384]{3,2,1,0:T(8,128)(2,1)}, bf16[4,24,256]{2,1,0:T(8,128)(2,1)}, bf16[4,2,64,432]{3,2,1,0:T(8,128)(2,1)}, bf16[4,2,48,1152]{3,2,1,0:T(8,128)(2,1)}, f32[4,1,128]{2,1,0:T(1,128)}) custom-call(bf16[4,24,384]{2,1,0:T(8,128)(2,1)} %pad_maximum_fusion.refs_0_, bf16[4,24,256]{2,1,0:T(8,128)(2,1)} %bitcast.55, ...), custom_call_target="tpu_custom_call" | custom-call | tf_op jit(solution)/shard_map/gather_inputs/pallas_call | solution.py:131
  34.3 1.0 %copy.28 = bf16[3,4,24,384]{3,1,2,0:T(4,128)(2,1)S(1)} copy(bf16[3,4,24,384]{3,2,1,0:T(8,128)(2,1)} %get-tuple-element.14) | data formatting | bytes 442368 | tf_op jit(solution)/shard_map/gather_inputs/pallas_call | solution.py:131
  35.4 0.1 reshape.96
  35.5 0.8 broadcast_select_fusion.refs_0_
  36.3 0.8 copy.30
  37.1 0.6 copy.32.refs_1_
  37.8 0.0 copy-done.6
  37.8 0.7 reshape.101.refs_5_
  38.4 0.0 copy-done.1
  38.4 0.6 multiply_subtract_fusion
  39.0 0.0 copy-start.5
  39.1 2.9 %fusion = (bf16[1024,1024]{1,0:T(8,128)(2,1)}, bf16[1024,1024]{1,0:T(8,128)(2,1)}) fusion(f32[32,32,1024]{2,1,0:T(8,128)S(1)} %multiply_subtract_fusion), kind=kLoop, calls=%fused_computation.2 | loop fusion | flops 4194304 | bytes 8388608 | tf_op jit(solution)/shard_map/convert_element_type | solution.py:441
  41.9 1.3 %dynamic-slice_bitcast_fusion.1 = (f32[4,128]{1,0:T(4,128)}, f32[1,4,128]{2,1,0:T(4,128)S(1)}) fusion(f32[16,4,128]{2,1,0:T(4,128)} %constant.80.clone, s32[]{:T(128)S(6)} %select_n.26), kind=kLoop, calls=%fused_computation.23 | loop fusion | bytes 6148 | tf_op jit(solution)/shard_map/jit(dynamic_index_in_dim)/squeeze | solution.py:509
  43.2 0.0 copy-done
  43.2 0.1 dynamic-slice_bitcast_fusion
  43.3 0.1 multiply_add_fusion
  43.4 0.6 pad_maximum_fusion.1.refs_13_
  44.0 0.8 jit_solution_.3.refs_14_
  44.8 51.6 %couple_and_solve.1 = f32[2,24,1024]{2,1,0:T(8,128)} custom-call(bf16[6,48,384]{2,1,0:T(8,128)(2,1)} %broadcast_select_fusion.refs_0_, bf16[2,48,256]{2,1,0:T(8,128)(2,1)} %copy.32.refs_1_, bf16[4,128,432]{2,1,0:T(8,128)(2,1)} %bitcast.53, bf16[4,96,1152]{2,1,0:T(8,128)(2,1)} %bitcast.50, f32[4,1,128]{2,1,0:T(1,128)} %get-tuple-element.18.refs_4_, ...), custom_call_target="tpu_custom_call" | custom-call | tf_op jit(solution)/shard_map/couple_and_solve/pallas_call | solution.py:414
  96.4 1.6 %copy.45 = f32[2,24,1024]{2,1,0:T(8,128)} copy(f32[2,24,1024]{2,1,0:T(8,128)} %couple_and_solve.1) | data formatting | bytes 393216
  (16 shorter events, 0.2 us)
Async XLA Ops:
  0.0 43.2 %copy-start = (f32[3,3,96]{2,1,0:T(4,128)S(1)}, f32[3,3,96]{2,1,0:T(4,128)}, u32[]{:S(2)}) copy-start(f32[3,3,96]{2,1,0:T(4,128)} %param.25) | copy-start | bytes 10372
  0.0 38.4 %copy-start.1 = (f32[32,1024]{1,0:T(8,128)S(1)}, f32[32,1024]{1,0:T(8,128)}, u32[]{:S(2)}) copy-start(f32[32,1024]{1,0:T(8,128)} %constant.76.clone) | copy-start | bytes 393220
  0.0 38.4 %copy-start.2 = (f32[32,1024]{1,0:T(8,128)S(1)}, f32[32,1024]{1,0:T(8,128)}, u32[]{:S(2)}) copy-start(f32[32,1024]{1,0:T(8,128)} %constant.77.clone) | copy-start | bytes 393220
  0.0 38.4 %copy-start.3 = (f32[32,1024]{1,0:T(8,128)S(1)}, f32[32,1024]{1,0:T(8,128)}, u32[]{:S(2)}) copy-start(f32[32,1024]{1,0:T(8,128)} %constant.78.clone) | copy-start | bytes 393220
  0.0 38.4 %copy-start.4 = (f32[32,1024]{1,0:T(8,128)S(1)}, f32[32,1024]{1,0:T(8,128)}, u32[]{:S(2)}) copy-start(f32[32,1024]{1,0:T(8,128)} %constant.79.clone) | copy-start | bytes 393220
  0.0 37.7 %copy-start.6 = (f32[2,48]{1,0:T(2,128)S(1)}, f32[2,48]{1,0:T(2,128)}, u32[]{:S(2)}) copy-start(f32[2,48]{1,0:T(2,128)} %param.23) | copy-start | bytes 1156
  39.0 4.9 %copy-start.5 = (f32[2,256]{1,0:T(2,128)S(1)}, f32[2,256]{1,0:T(2,128)}, u32[]{:S(2)}) copy-start(f32[2,256]{1,0:T(2,128)} %constant.85.clone) | copy-start | bytes 6148

commit v5 on v4

--- a/solution.py
+++ b/solution.py
@@ -13,10 +13,15 @@
 mesh_ids = pl.DeviceIdType.MESH
 
 
+def split(values):
+    high = values.astype(jnp.bfloat16)
+    return high, (values - high.astype(jnp.float32)).astype(jnp.bfloat16)
+
+
 def gather_kernel(rows, chans, halves_of, *refs):
-    za_ref, zb_ref, win_ref, wout_ref, bias_ref = refs[:5]
-    za_out, zb_out, win_out, wout_out, bias_out = refs[5:10]
-    za_sems, zb_sems, w_sems, pass_sems, own_sem = refs[10:]
+    za_ref, zb_ref, win_ref, wout_ref, bias_ref, turn_ref = refs[:6]
+    za_out, zb_out, win_out, wout_out, bias_out, high_out, low_out = refs[6:13]
+    za_sems, zb_sems, w_sems, pass_sems, own_sem = refs[13:]
     me_row = lax.axis_index("rows")
     me_chan = lax.axis_index("chan")
     core = lax.rem(me_row, 2)
@@ -95,6 +100,18 @@
         one.start()
     for one in copies:
         one.start()
+    fine = turn_ref.shape[1]
+
+    def fill(outer, carry):
+        at = pl.ds(outer, 1)
+        values = turn_ref[0, at, :] * turn_ref[2] - turn_ref[1, at, :] * turn_ref[3]
+        high, low = split(values)
+        here = pl.ds(pl.multiple_of(outer * fine, fine), fine)
+        high_out[here, :] = high
+        low_out[here, :] = low
+        return carry
+
+    lax.fori_loop(0, high_out.shape[0] // fine, fill, 0)
     passed = []
     for idx, step in enumerate(steps):
         origin = lax.rem(spot + ring - step, ring)
@@ -121,7 +138,7 @@
         one.wait_send()
 
 
-def gather(za_cols, zb_cols, w_in, w_out, bias, rows, chans, halves_of):
+def gather(za_cols, zb_cols, w_in, w_out, bias, turns, rows, chans, halves_of):
     def kernel(*refs):
         gather_kernel(rows, chans, halves_of, *refs)
 
@@ -136,9 +153,11 @@
             several((chans,), w_in),
             several((chans,), w_out),
             several((chans,), bias),
+            jax.ShapeDtypeStruct((turns.shape[2],) * 2, jnp.bfloat16),
+            jax.ShapeDtypeStruct((turns.shape[2],) * 2, jnp.bfloat16),
         ),
-        in_specs=[vmem] * 5,
-        out_specs=(vmem,) * 5,
+        in_specs=[vmem] * 6,
+        out_specs=(vmem,) * 7,
         scratch_shapes=[
             pltpu.SemaphoreType.DMA((2, 3 * chans)),
             pltpu.SemaphoreType.DMA((2, 2, chans)),
@@ -148,7 +167,7 @@
         ],
         compiler_params=pltpu.CompilerParams(collective_id=0, has_side_effects=True),
         name="gather_inputs",
-    )(za_cols, zb_cols, w_in, w_out, bias)
+    )(za_cols, zb_cols, w_in, w_out, bias, turns)
 
 
 def as_column(line):
@@ -158,15 +177,21 @@
     return jnp.sum(jnp.where(down == along, line, 0.0), axis=1, keepdims=True)
 
 
-def couple_kernel(dims, refs, taps_ref, hidden_ref):
+def couple_kernel(dims, refs, plane_ref, latent_ref, taps_ref, hidden_ref):
     slab, half, quarter, hidden_local, groups, block, width, height = dims
     za_ref, zb_ref, win_ref, wout_ref, bias_ref, bout_ref, unmix_ref, out_ref = refs
-    wide = za_ref.shape[2]
+    wide = za_ref.shape[3]
     first_row = lax.axis_index("rows") * slab - slab
     first_col = lax.axis_index("chan") * block - 1
     span = 3 * half
     for row in range(3 * slab):
-        plane = za_ref[row].astype(jnp.float32)
+        line = first_row + row
+        held = (line >= 0) & (line < height)
+        for part in range(groups):
+            piece = za_ref[row // slab, part].astype(jnp.float32)
+            piece = piece[row % slab * quarter : (row % slab + 1) * quarter]
+            plane_ref[row, pl.ds(part * quarter, quarter), :] = jnp.where(held, piece, 0.0)
+        plane = plane_ref[row]
         for off in range(3):
             moved = plane if off == 0 else pltpu.roll(plane, wide - off, 1)
             taps_ref[pl.ds(row * span + off * half, half), :] = moved.astype(jnp.bfloat16)
@@ -174,7 +199,7 @@
     inside = (cols >= 0) & (cols < width)
     deep = 3 * hidden_local
     biases = [as_column(bias_ref[part]) for part in range(groups)]
-    out_bias = as_column(bout_ref[...])
+    out_bias = jnp.concatenate([as_column(bout_ref[pl.ds(i, 1), :]) for i in range(2)], axis=0)
     for row in range(2 * slab):
         line = first_row + row + 1
         keep = inside & (line >= 0) & (line < height)
@@ -199,9 +224,12 @@
                 hidden_ref[part, pl.ds(row * deep, 3 * deep), :],
                 preferred_element_type=jnp.float32,
             )
-        latent = zb_ref[row].astype(jnp.float32)
+        for part in range(groups):
+            piece = zb_ref[part].astype(jnp.float32)[row * quarter : (row + 1) * quarter]
+            latent_ref[row, pl.ds(part * quarter, quarter), :] = piece
+        latent = latent_ref[row]
         coupled = (latent - raw[half:]) * jnp.exp(-jnp.tanh(raw[:half]))
-        own = pltpu.roll(za_ref[slab + row].astype(jnp.float32), wide - 2, 1)[:, :block]
+        own = pltpu.roll(plane_ref[slab + row], wide - 2, 1)[:, :block]
         joined = jnp.concatenate([own, coupled], axis=0)
         mixed = jnp.dot(
             unmix_ref[...],
@@ -213,19 +241,15 @@
             out_ref[part, pl.ds(row * share, share), :] = mixed[part * share : (part + 1) * share]
 
 
-def split(values):
-    high = values.astype(jnp.bfloat16)
-    return high, (values - high.astype(jnp.float32)).astype(jnp.bfloat16)
-
-
 def main_kernel(dims, counts, *refs):
     slab, half, quarter, hidden_local, groups, block, width, height = dims
     rows, triple, lanes = counts
     couple_refs = refs[:7]
     thigh_ref, tlow_ref, fhigh_ref, flow_ref, bhigh_ref, blow_ref = refs[7:13]
-    near_ref, turn_ref, lane_ref, out_ref = refs[13:17]
-    taps_ref, hidden_ref, mix_ref, mixed_ref, send_ref, got_ref, back_ref, home_ref = refs[17:25]
-    work_ref, own_sem, chan_sem, there_sem, back_sem = refs[25:]
+    kern_ref, turn_ref, lane_ref, out_ref = refs[13:17]
+    plane_ref, latent_ref, taps_ref, hidden_ref, kern_cols = refs[17:22]
+    mix_ref, mixed_ref, send_ref, got_ref, back_ref, home_ref = refs[22:28]
+    work_ref, own_sem, chan_sem, there_sem, back_sem = refs[28:]
     mine = 2 * half // groups
     tile = 2 * lanes
     freq_groups = width // lanes
@@ -251,7 +275,16 @@
             device_id_type=mesh_ids,
         )
     lax.fori_loop(1, rows, greet, 0)
-    couple_kernel(dims, tuple(couple_refs) + (mix_ref,), taps_ref, hidden_ref)
+    couple_kernel(
+        dims, tuple(couple_refs) + (mix_ref,), plane_ref, latent_ref, taps_ref, hidden_ref
+    )
+    at = lax.broadcasted_iota(jnp.int32, kern_cols.shape, 1)
+    spread = jnp.zeros(kern_cols.shape, jnp.float32)
+    for row_off in range(3):
+        for col_off in range(3):
+            column = as_column(kern_ref[row_off, pl.ds(col_off, 1), :])
+            spread = jnp.where(at == 3 * row_off + col_off, column, spread)
+    kern_cols[...] = spread
     pl.semaphore_wait(barrier, rows - 1 + groups - 1)
 
     swaps = []
@@ -323,8 +356,12 @@
     exchange(send_ref, got_ref, there_sem, 1)
 
     lane = lax.broadcasted_iota(jnp.int32, (rows, tile), 1)
-    sign = lane_ref[pl.ds(0, 1), :]
-    scale = lane_ref[pl.ds(1, 1), :]
+    lane_table = lane_ref[me_row // chan_groups]
+    sign = lane_table[0:1]
+    scale = lane_table[1:2]
+    cos_v = lane_table[2:3]
+    sin_v = lane_table[3:4]
+    chan_first = me_chan * mine + lax.rem(me_row, chan_groups) * triple
     stacks = []
     for chan in range(triple):
         data = got_ref[:, chan, :]
@@ -338,15 +375,18 @@
     forward = jnp.dot(fhigh_ref[...], high, preferred_element_type=jnp.float32)
     forward = forward + jnp.dot(fhigh_ref[...], low, preferred_element_type=jnp.float32)
     forward = forward + jnp.dot(flow_ref[...], high, preferred_element_type=jnp.float32)
-    cos_u = turn_ref[0]
-    sin_u = turn_ref[1]
+    cos_u = as_column(turn_ref[pl.ds(0, 1), :])
+    sin_u = as_column(turn_ref[pl.ds(1, 1), :])
     solved = []
     for chan in range(triple):
         piece = forward[:, chan * tile : (chan + 1) * tile]
         parts = [piece[i * height : (i + 1) * height] for i in range(4)]
         real_part = parts[0] + pltpu.roll(parts[1], lanes, 1)
         imag_part = parts[2] + pltpu.roll(parts[3], lanes, 1)
-        near = [near_ref[i, pl.ds(chan, 1), :] for i in range(6)]
+        stencil = kern_cols[pl.ds(chan_first + chan, 1), :]
+        taps = [stencil[:, i : i + 1] for i in range(9)]
+        near = [taps[3 * i + 1] + (taps[3 * i] + taps[3 * i + 2]) * cos_v for i in range(3)]
+        near += [(taps[3 * i + 2] - taps[3 * i]) * sin_v for i in range(3)]
         symbol_real = near[1] + (near[0] + near[2]) * cos_u + (near[3] - near[5]) * sin_u
         symbol_imag = near[4] + (near[3] + near[5]) * cos_u + (near[2] - near[0]) * sin_u
         factor = scale / (symbol_real * symbol_real + symbol_imag * symbol_imag)
@@ -402,7 +442,7 @@
 def whole(operands, dims, counts):
     slab, half, quarter, hidden_local, groups, block, width, height = dims
     rows, triple, lanes = counts
-    wide = operands[0].shape[2]
+    wide = operands[0].shape[3]
     mine = 2 * half // groups
     tile = 2 * lanes
 
@@ -417,8 +457,11 @@
         in_specs=[vmem] * len(operands),
         out_specs=vmem,
         scratch_shapes=[
+            pltpu.VMEM((3 * slab, half, wide), jnp.float32),
+            pltpu.VMEM((slab, half, block), jnp.float32),
             pltpu.VMEM((3 * slab * 3 * half, wide), jnp.bfloat16),
             pltpu.VMEM((groups, 2 * slab * 3 * hidden_local, block), jnp.bfloat16),
+            pltpu.VMEM((2 * half, tile), jnp.float32),
             mix,
             mix,
             message,
@@ -436,11 +479,6 @@
     )(*operands)
 
 
-def halves(values):
-    high = lax.reduce_precision(values, 8, 7)
-    return high.astype(jnp.bfloat16), (values - high).astype(jnp.bfloat16)
-
-
 def column_tables(width, group):
     pos = np.arange(width)
     part = pos // group % 2
@@ -451,13 +489,10 @@
     fine = 32
     outer = (np.arange(width // fine) * fine)[:, None] * freq[None, :] % width * (full_turn / width)
     inner = np.arange(fine)[:, None] * freq[None, :] % width * (full_turn / width) + shift[None, :]
-    consts = [f(a).astype(np.float32) for a in (outer, inner) for f in (np.cos, np.sin)]
-    cos_o, sin_o, cos_i, sin_i = lax.optimization_barrier(tuple(jnp.asarray(c) for c in consts))
-    table = cos_o[:, None, :] * cos_i[None] - sin_o[:, None, :] * sin_i[None]
-    table = table.reshape(width, width)
+    turns = np.stack([f(a) for a in (outer, inner) for f in (np.cos, np.sin)])
     sign = np.where(first, 0.0, 1.0 - 2.0 * part).astype(np.float32)
     weight = np.where(first, 1.0, 2.0).astype(np.float32)
-    return halves(table), freq, sign, weight
+    return turns.astype(np.float32), freq, sign, weight
 
 
 def on_device(za, zb, w_in, b_in, w_out, b_out, unmix, kern):
@@ -467,8 +502,6 @@
     half = chans // 2
     rows = lax.axis_size("rows")
     groups = lax.axis_size("chan")
-    row_idx = lax.axis_index("rows")
-    chan_idx = lax.axis_index("chan")
     height = slab * rows
     block = width // groups
     mine = chans // groups
@@ -477,7 +510,7 @@
     chan_groups = rows // freq_groups
     triple = mine // chan_groups
 
-    table, freq, sign, weight = column_tables(width, lanes // 2)
+    col_turns, freq, sign, weight = column_tables(width, lanes // 2)
 
     zb_cols = zb.reshape(slab * quarter, groups, block).transpose(1, 0, 2)
     za_wide = jnp.pad(za.reshape(slab * quarter, width), ((0, 0), (2, 128 + 2)))
@@ -491,31 +524,15 @@
     w_out_parts = w_out.reshape(taps * hidden_local, chans).T.reshape(
         2, chans // 2, taps * hidden_local
     )
-    za_got, zb_got, w_in_all, w_out_all, bias = gather(
-        za_cols, zb_cols, w_in_parts, w_out_parts, b_in[None, :], rows, groups, 2
-    )
-    za_ext = za_got.reshape(3, groups, slab, quarter, block + 128)
-    za_ext = za_ext.transpose(0, 2, 1, 3, 4).reshape(3 * slab, half, block + 128)
-    ext_rows = row_idx * slab - slab + jnp.arange(3 * slab, dtype=jnp.int32)
-    inside = (ext_rows >= 0) & (ext_rows < height)
-    za_ext = jnp.where(inside[:, None, None], za_ext, jnp.zeros((), za.dtype))
-    latent = zb_got.reshape(groups, slab, quarter, block).transpose(1, 0, 2, 3)
-    freq_idx = row_idx // chan_groups
-    chan_first = chan_idx * mine + row_idx % chan_groups * triple
+    za_got, zb_got, w_in_all, w_out_all, bias, *table = gather(
+        za_cols, zb_cols, w_in_parts, w_out_parts, b_in[None, :], jnp.asarray(col_turns), rows, groups, 2
+    )
     turn = freq * (full_turn / width)
     lane_rows = np.stack([sign, weight * (1.0 / (height * width)), np.cos(turn), np.sin(turn)])
     lane_rows = lane_rows.astype(np.float32).reshape(4, freq_groups, lanes).transpose(1, 0, 2)
     lane_rows = np.concatenate([lane_rows, lane_rows], axis=2)
-    lane_own = lax.dynamic_index_in_dim(jnp.asarray(lane_rows), freq_idx, 0, keepdims=False)
-    cos_v = lane_own[2][None, None, :]
-    sin_v = lane_own[3][None, None, :]
-    stencil = lax.dynamic_slice_in_dim(kern, chan_first, triple, 2)[..., None]
-    near_real = stencil[:, 1] + (stencil[:, 0] + stencil[:, 2]) * cos_v
-    near_imag = (stencil[:, 2] - stencil[:, 0]) * sin_v
-    near = jnp.concatenate([near_real, near_imag], axis=0)
     row_turn = np.arange(height) * (full_turn / height)
     turns = np.stack([np.cos(row_turn), np.sin(row_turn)]).astype(np.float32)
-    turns = np.broadcast_to(turns[:, :, None], (2, height, 2 * lanes))
 
     blocks = []
     for row in range(slab):
@@ -533,19 +550,19 @@
         return jnp.asarray(high), jnp.asarray(low)
 
     operands = (
-        za_ext,
-        latent.reshape(slab, half, block),
+        za_got,
+        zb_got,
         w_in_all.reshape(groups, hidden_local, taps * half),
         w_out_all.reshape(groups, chans, taps * hidden_local),
         bias,
-        b_out.reshape(1, chans),
+        b_out,
         unmix,
         *table,
         *fixed(ahead),
         *fixed(behind),
-        near,
+        kern,
         jnp.asarray(turns),
-        lane_own,
+        jnp.asarray(lane_rows),
     )
     dims = (slab, half, quarter, hidden_local, groups, block, width, height)
     return whole(operands, dims, (rows, triple, lanes))

time: 99.7 us -> 90.5 us (0.908)
  local copies, waits for them, and re-layouts: 13.2 us -> 7.62 us
  other arithmetic: 5.62 us -> 0.65 us
  Pallas kernels: 79.1 us -> 80.6 us
    convert_element_type x1 -> x0, other arithmetic: 2.87 us -> none  [halves(): return (high.astype(jnp.bfloat16), (values - high).astype(jnp.bfloat16))]
    pallas_call x2 -> x0, local copies, waits for them, and re-layouts: 1.84 us -> none  [gather(): pl.pallas_call(kernel, out_shape=(several((3,), za_cols), several((), zb_...]
    pallas_call x1, Pallas kernels: 27.5 us -> 29 us  [gather(): pl.pallas_call(kernel, out_shape=(several((3,), za_cols), several((), zb_...]
    reshape x3 -> x0, local copies, waits for them, and re-layouts: 1.33 us -> none  [the longest x1 0.65 us: on_device(): b_out.reshape(1, chans)]
    squeeze x1 -> x0, local copies, waits for them, and re-layouts: 1.26 us -> none  [on_device(): lax.dynamic_index_in_dim(jnp.asarray(lane_rows), freq_idx, 0, keepdims=Fa...]
    unnamed x21 -> x4, local copies, waits for them, and re-layouts: 4.46 us -> 4.32 us
where the time goes in v5:
time: 90.5 us; the launch traced here: 88.9 us
  Pallas kernels  80.6 us (89%)
  local copies, waits for them, and re-layouts  7.62 us (8%)
    pallas_call x1, Pallas kernels, whole(): pl.pallas_call(kernel, out_shape=jax.ShapeDtypeStruct((slab, mine, width)...  51.6 us
    pallas_call x1, Pallas kernels, gather(): pl.pallas_call(kernel, out_shape=(several((3,), za_cols), several((), zb_...  29 us
    unnamed x4, local copies, waits for them, and re-layouts  4.32 us

profile of v5, /device:TPU:1, one launch (start us, length us, event | category | flops | bytes accessed | tf_op | source)
XLA Modules:
  0.0 88.9 jit_solution(16091625452980700626)
XLA Ops:
  0.0 0.8 copy.18
  0.8 0.1 fusion
  0.9 0.7 pad_maximum_fusion.refs_0_
  1.6 0.8 copy.19
  2.4 0.6 copy.24
  3.1 1.7 %copy.21 = bf16[432,128]{0,1:T(8,128)(2,1)} copy(bf16[432,128]{1,0:T(8,128)(2,1)} %bitcast.28) | data formatting | bytes 221184 | tf_op jit(solution)/shard_map/reshape | solution.py:521
  4.7 1.1 %copy.22 = bf16[3,3,128,2,48]{2,1,0,4,3:T(4,128)(2,1)S(1)} copy(bf16[3,3,128,2,48]{2,4,3,1,0:T(8,128)(2,1)} %param.19) | data formatting | bytes 442368 | tf_op args[4]
  5.8 0.9 reshape.28
  6.7 29.0 %gather_inputs.1 = (bf16[3,4,24,384]{3,2,1,0:T(8,128)(2,1)}, bf16[4,24,256]{2,1,0:T(8,128)(2,1)}, bf16[4,2,64,432]{3,2,1,0:T(8,128)(2,1)}, bf16[4,2,48,1152]{3,2...) custom-call(bf16[4,24,384]{2,1,0:T(8,128)(2,1)} %pad_maximum_fusion.refs_0_, ...), custom_call_target="tpu_custom_call" | custom-call | tf_op jit(solution)/shard_map/gather_inputs/pallas_call | solution.py:148
  35.7 51.6 %couple_and_solve.1 = f32[2,24,1024]{2,1,0:T(8,128)} custom-call(bf16[3,4,24,384]{3,2,1,0:T(8,128)(2,1)} %get-tuple-element.12.refs_0_, bf16[4,24,256]{2,1,0:T(8,128)(2,1)} %get-tuple-element.13.refs_1_, bf16[4,128,432]{2,1,0:T(8,128)(2,1)} %bitcast.25, bf16[4,96,1152]{2,1,0:T(8,128)(2,1)} %bitcast.23, f32[4,1,128]{2,1,0:T(1,128)} %get-tuple-element.16.refs_4_, ...), custom_call_target="tpu_custom_call" | custom-call | tf_op jit(solution)/shard_map/couple_and_solve/pallas_call | solution.py:454
  87.3 1.6 %copy.26 = f32[2,24,1024]{2,1,0:T(8,128)} copy(f32[2,24,1024]{2,1,0:T(8,128)} %couple_and_solve.1) | data formatting | bytes 393216
  (2 shorter events, 0.0 us)

commit v6 on v5

--- a/solution.py
+++ b/solution.py
@@ -198,6 +198,10 @@
     cols = first_col + lax.broadcasted_iota(jnp.int32, (hidden_local, wide), 1)
     inside = (cols >= 0) & (cols < width)
     deep = 3 * hidden_local
+    weights = []
+    for part in range(groups):
+        joint = jnp.concatenate([win_ref[part, i].astype(jnp.float32) for i in range(2)], axis=0)
+        weights.append(joint.T.astype(jnp.bfloat16))
     biases = [as_column(bias_ref[part]) for part in range(groups)]
     out_bias = jnp.concatenate([as_column(bout_ref[pl.ds(i, 1), :]) for i in range(2)], axis=0)
     for row in range(2 * slab):
@@ -206,7 +210,7 @@
         stack = taps_ref[pl.ds(row * span, 3 * span), :]
         for part in range(groups):
             value = lax.dot_general(
-                win_ref[part], stack, (((1,), (0,)), ((), ())), preferred_element_type=jnp.float32
+                weights[part], stack, (((1,), (0,)), ((), ())), preferred_element_type=jnp.float32
             )
             value = jnp.maximum(value + biases[part], 0.0)
             value = jnp.where(keep, value, 0.0)
@@ -239,6 +243,10 @@
         )
         for part in range(groups):
             out_ref[part, pl.ds(row * share, share), :] = mixed[part * share : (part + 1) * share]
+
+
+def outward(turn, count):
+    return count // 2 + (turn + 1) // 2 * (1 - 2 * lax.rem(turn, 2))
 
 
 def main_kernel(dims, counts, *refs):
@@ -258,7 +266,8 @@
     me_chan = lax.axis_index("chan")
     barrier = pltpu.get_barrier_semaphore()
 
-    def greet(step, carry):
+    def greet(turn, carry):
+        step = outward(turn, rows)
         pl.semaphore_signal(
             barrier,
             inc=1,
@@ -274,7 +283,7 @@
             device_id=(me_row, lax.rem(me_chan + step, groups)),
             device_id_type=mesh_ids,
         )
-    lax.fori_loop(1, rows, greet, 0)
+    lax.fori_loop(0, rows - 1, greet, 0)
     couple_kernel(
         dims, tuple(couple_refs) + (mix_ref,), plane_ref, latent_ref, taps_ref, hidden_ref
     )
@@ -339,15 +348,15 @@
                 device_id_type=mesh_ids,
             )
 
-        def start(step, carry):
-            copy(step).start()
+        def start(turn, carry):
+            copy(outward(turn, rows)).start()
             return carry
 
         def finish(step, carry):
             copy(step).wait()
             return carry
 
-        lax.fori_loop(1, rows, start, 0)
+        lax.fori_loop(0, rows - 1, start, 0)
         kept = pltpu.make_async_copy(source.at[me_row], target.at[me_row], own_sem.at[own_at])
         kept.start()
         kept.wait()
@@ -518,9 +527,7 @@
         [za_wide[:, block * i : block * i + block + 128] for i in range(groups)], axis=0
     )
     taps = 9
-    w_in_parts = w_in.reshape(taps * half, hidden_local).T.reshape(
-        2, hidden_local // 2, taps * half
-    )
+    w_in_parts = w_in.reshape(2, taps * half // 2, hidden_local)
     w_out_parts = w_out.reshape(taps * hidden_local, chans).T.reshape(
         2, chans // 2, taps * hidden_local
     )
@@ -552,7 +559,7 @@
     operands = (
         za_got,
         zb_got,
-        w_in_all.reshape(groups, hidden_local, taps * half),
+        w_in_all,
         w_out_all.reshape(groups, chans, taps * hidden_local),
         bias,
         b_out,

time: 90.5 us -> 89.3 us (0.987)
  local copies, waits for them, and re-layouts: 7.62 us -> 5.98 us
  Pallas kernels: 80.6 us -> 81.7 us
    reshape x1 -> x0, local copies, waits for them, and re-layouts: 1.66 us -> none  [on_device(): w_in.reshape(taps * half, hidden_local)]
    pallas_call x1, Pallas kernels: 51.6 us -> 53.2 us  [whole(): pl.pallas_call(kernel, out_shape=jax.ShapeDtypeStruct((slab, mine, width)...]
where the time goes in v6:
time: 89.3 us; the launch traced here: 88.4 us
  Pallas kernels  81.7 us (91%)
  local copies, waits for them, and re-layouts  5.98 us (7%)
    pallas_call x1, Pallas kernels, whole(): pl.pallas_call(kernel, out_shape=jax.ShapeDtypeStruct((slab, mine, width)...  53.2 us
    pallas_call x1, Pallas kernels, gather(): pl.pallas_call(kernel, out_shape=(several((3,), za_cols), several((), zb_...  28.5 us
    unnamed x4, local copies, waits for them, and re-layouts  4.32 us

profile of v6, /device:TPU:1, one launch (start us, length us, event | category | flops | bytes accessed | tf_op | source)
XLA Modules:
  0.0 88.4 jit_solution(11562821242466589380)
XLA Ops:
  0.0 0.8 copy.17
  0.8 0.1 fusion
  0.9 0.6 pad_maximum_fusion.refs_0_
  1.6 0.8 copy.18
  2.4 0.6 copy.22
  3.1 1.1 %copy.20 = bf16[3,3,128,2,48]{2,1,0,4,3:T(4,128)(2,1)S(1)} copy(bf16[3,3,128,2,48]{2,4,3,1,0:T(8,128)(2,1)} %param.19) | data formatting | bytes 442368 | tf_op args[4]
  4.2 0.9 %reshape.21 = bf16[1152,96]{0,1:T(8,128)(2,1)} reshape(bf16[3,3,128,2,48]{2,1,0,4,3:T(4,128)(2,1)S(1)} %copy.20) | data formatting | bytes 442368 | tf_op jit(solution)/shard_map/reshape | solution.py:531
  5.0 28.5 %gather_inputs.1 = (bf16[3,4,24,384]{3,2,1,0:T(8,128)(2,1)}, bf16[4,24,256]{2,1,0:T(8,128)(2,1)}, bf16[4,2,216,128]{3,2,1,0:T(8,128)(2,1)}, bf16[4,2,48,1152]{3,...) custom-call(bf16[4,24,384]{2,1,0:T(8,128)(2,1)} %pad_maximum_fusion.refs_0_, ...), custom_call_target="tpu_custom_call" | custom-call | tf_op jit(solution)/shard_map/gather_inputs/pallas_call | solution.py:148
  33.6 53.2 %couple_and_solve.1 = f32[2,24,1024]{2,1,0:T(8,128)} custom-call(bf16[3,4,24,384]{3,2,1,0:T(8,128)(2,1)} %get-tuple-element.12.refs_0_, bf16[4,24,256]{2,1,0:T(8,128)(2,1)} %get-tuple-element.13.refs_1_, bf16[4,2,216,128]{3,2,1,0:T(8,128)(2,1)} %get-tuple-element.14.refs_2_, bf16[4,96,1152]{2,1,0:T(8,128)(2,1)} %bitcast.19, ...), custom_call_target="tpu_custom_call" | custom-call | tf_op jit(solution)/shard_map/couple_and_solve/pallas_call | solution.py:463
  86.8 1.6 %copy.24 = f32[2,24,1024]{2,1,0:T(8,128)} copy(f32[2,24,1024]{2,1,0:T(8,128)} %couple_and_solve.1) | data formatting | bytes 393216
  (2 shorter events, 0.0 us)

commit v7 on v6

--- a/solution.py
+++ b/solution.py
@@ -40,6 +40,10 @@
         there = lax.rem(spot + step, ring)
         return (me_row + (there // chans - side) * 2, lax.rem(there, chans))
 
+    def zb_block(peer):
+        block = zb_out.shape[3]
+        return zb_ref.at[:, :, pl.ds(pl.multiple_of(peer * block, block), block)]
+
     for step in steps:
         pl.semaphore_signal(
             barrier, inc=1, device_id=around(ring - step), device_id_type=mesh_ids
@@ -50,7 +54,7 @@
         pltpu.make_async_copy(win_ref, win_out.at[me_chan], own_sem.at[0]),
         pltpu.make_async_copy(wout_ref, wout_out.at[me_chan], own_sem.at[1]),
         pltpu.make_async_copy(za_ref.at[me_chan], za_out.at[1, me_chan], own_sem.at[2]),
-        pltpu.make_async_copy(zb_ref.at[me_chan], zb_out.at[me_chan], own_sem.at[3]),
+        pltpu.make_async_copy(zb_block(me_chan), zb_out.at[me_chan], own_sem.at[3]),
         pltpu.make_async_copy(bias_ref, bias_out.at[me_chan], own_sem.at[4]),
     ]
     for one in own:
@@ -84,7 +88,7 @@
         )
     for dc in range(1, chans):
         peer = lax.rem(me_chan + dc, chans)
-        pairs = ((zb_ref.at[peer], zb_out), (bias_ref, bias_out))
+        pairs = ((zb_block(peer), zb_out), (bias_ref, bias_out))
         for kind, (source, target) in enumerate(pairs):
             copies.append(
                 pltpu.make_async_remote_copy(
@@ -138,7 +142,7 @@
         one.wait_send()
 
 
-def gather(za_cols, zb_cols, w_in, w_out, bias, turns, rows, chans, halves_of):
+def gather(za_cols, zb_turned, w_in, w_out, bias, turns, rows, chans, halves_of):
     def kernel(*refs):
         gather_kernel(rows, chans, halves_of, *refs)
 
@@ -149,7 +153,9 @@
         kernel,
         out_shape=(
             several((3,), za_cols),
-            several((), zb_cols),
+            jax.ShapeDtypeStruct(
+                (chans,) + zb_turned.shape[:2] + (zb_turned.shape[2] // chans,), zb_turned.dtype
+            ),
             several((chans,), w_in),
             several((chans,), w_out),
             several((chans,), bias),
@@ -167,7 +173,7 @@
         ],
         compiler_params=pltpu.CompilerParams(collective_id=0, has_side_effects=True),
         name="gather_inputs",
-    )(za_cols, zb_cols, w_in, w_out, bias, turns)
+    )(za_cols, zb_turned, w_in, w_out, bias, turns)
 
 
 def as_column(line):
@@ -229,7 +235,7 @@
                 preferred_element_type=jnp.float32,
             )
         for part in range(groups):
-            piece = zb_ref[part].astype(jnp.float32)[row * quarter : (row + 1) * quarter]
+            piece = zb_ref[part].astype(jnp.float32)[:, row, :]
             latent_ref[row, pl.ds(part * quarter, quarter), :] = piece
         latent = latent_ref[row]
         coupled = (latent - raw[half:]) * jnp.exp(-jnp.tanh(raw[:half]))
@@ -521,7 +527,7 @@
 
     col_turns, freq, sign, weight = column_tables(width, lanes // 2)
 
-    zb_cols = zb.reshape(slab * quarter, groups, block).transpose(1, 0, 2)
+    zb_turned = zb.transpose(1, 0, 2)
     za_wide = jnp.pad(za.reshape(slab * quarter, width), ((0, 0), (2, 128 + 2)))
     za_cols = jnp.stack(
         [za_wide[:, block * i : block * i + block + 128] for i in range(groups)], axis=0
@@ -532,7 +538,7 @@
         2, chans // 2, taps * hidden_local
     )
     za_got, zb_got, w_in_all, w_out_all, bias, *table = gather(
-        za_cols, zb_cols, w_in_parts, w_out_parts, b_in[None, :], jnp.asarray(col_turns), rows, groups, 2
+        za_cols, zb_turned, w_in_parts, w_out_parts, b_in[None, :], jnp.asarray(col_turns), rows, groups, 2
     )
     turn = freq * (full_turn / width)
     lane_rows = np.stack([sign, weight * (1.0 / (height * width)), np.cos(turn), np.sin(turn)])

time: 89.3 us -> 87.8 us (0.983)
  local copies, waits for them, and re-layouts: 5.98 us -> 4.51 us
    unnamed x4 -> x3, local copies, waits for them, and re-layouts: 4.32 us -> 3.51 us
where the time goes in v7:
time: 87.8 us; the launch traced here: 87 us
  Pallas kernels  81.8 us (93%)
  local copies, waits for them, and re-layouts  4.51 us (5%)
    pallas_call x1, Pallas kernels, whole(): pl.pallas_call(kernel, out_shape=jax.ShapeDtypeStruct((slab, mine, width)...  53.3 us
    pallas_call x1, Pallas kernels, gather(): pl.pallas_call(kernel, out_shape=(several((3,), za_cols), jax.ShapeDtypeS...  28.5 us
    unnamed x3, local copies, waits for them, and re-layouts  3.51 us

profile of v7, /device:TPU:1, one launch (start us, length us, event | category | flops | bytes accessed | tf_op | source)
XLA Modules:
  0.0 87.0 jit_solution(17111357179034649866)
XLA Ops:
  0.0 0.8 copy.17
  0.8 0.1 fusion
  0.9 0.6 pad_maximum_fusion.refs_0_
  1.6 1.1 %copy.18 = bf16[3,3,128,2,48]{2,1,0,4,3:T(4,128)(2,1)S(1)} copy(bf16[3,3,128,2,48]{2,4,3,1,0:T(8,128)(2,1)} %param.19) | data formatting | bytes 442368 | tf_op args[4]
  2.7 0.9 %reshape.17 = bf16[1152,96]{0,1:T(8,128)(2,1)} reshape(bf16[3,3,128,2,48]{2,1,0,4,3:T(4,128)(2,1)S(1)} %copy.18) | data formatting | bytes 442368 | tf_op jit(solution)/shard_map/reshape | solution.py:537
  3.6 28.5 %gather_inputs.1 = (bf16[3,4,24,384]{3,2,1,0:T(8,128)(2,1)}, bf16[4,12,2,256]{3,2,1,0:T(2,128)(2,1)}, bf16[4,2,216,128]{3,2,1,0:T(8,128)(2,1)}, bf16[4,2,48,1152...) custom-call(bf16[4,24,384]{2,1,0:T(8,128)(2,1)} %pad_maximum_fusion.refs_0_, ...), custom_call_target="tpu_custom_call" | custom-call | tf_op jit(solution)/shard_map/gather_inputs/pallas_call | solution.py:152
  32.1 53.3 %couple_and_solve.1 = f32[2,24,1024]{2,1,0:T(8,128)} custom-call(bf16[3,4,24,384]{3,2,1,0:T(8,128)(2,1)} %get-tuple-element.12.refs_0_, bf16[4,12,2,256]{3,2,1,0:T(2,128)(2,1)} %get-tuple-element.13.refs_1_, bf16[4,2,216,128]{3,2,1,0:T(8,128)(2,1)} %get-tuple-element.14.refs_2_, bf16[4,96,1152]{2,1,0:T(8,128)(2,1)} %bitcast.17, ...), custom_call_target="tpu_custom_call" | custom-call | tf_op jit(solution)/shard_map/couple_and_solve/pallas_call | solution.py:469
  85.4 1.6 %copy.20 = f32[2,24,1024]{2,1,0:T(8,128)} copy(f32[2,24,1024]{2,1,0:T(8,128)} %couple_and_solve.1) | data formatting | bytes 393216
  (1 shorter events, 0.0 us)
